TPU v7x, 1024 devices: a whole 4x8x16 slice. The times are simulated.
1024 devices in a mesh: bx: 64 (over y, z_lo, core), by: 16 (over z_hi, x).
Axes of the slice: x: 4, y: 8, z: 16 (z_hi: 4, z_lo: 4; z = z_hi * 4 + z_lo), core: 2. Of those that a mesh axis runs over, the one named last changes fastest.
Arguments:
- populations: float32 [64, 16, 2, 19, 16, 256], P('bx', 'by'), may hold values from 0.019 to 0.467, as said below
- live_blocks: int32 [64, 16, 2], replicated, may hold values from 0 to 1, as said below
- moving: int32 [64, 16, 2], replicated, may hold values from 0 to 1, as said below
Outputs:
- final_populations: float32 [64, 16, 2, 19, 16, 256], P('bx', 'by')
Inputs may be any that keep to these rules, and one draw needn't show every extreme that they name: `populations`: each entry is a positive population between 0.7 and 1.4 times its lattice weight w_q. `live_blocks`: 1 marks a fluid block and 0 a solid one. `moving`: the devices with bx indices 2p and 2p + 1 and the same by index form a pair; 1 stands only on fluid blocks of the device of a pair that has more fluid blocks, and that device marks exactly half the difference of the two devices' fluid counts, rounded down.
All inputs are finite; a program needn't handle non-finite values.
Results may differ from a plain program's by a relative error of at most 0.0001.
Values sent between devices are 32-bit elements; how exact they have to be, the bound alone decides.
A program may use at most 32 MiB of HBM per device.

v0:
```python
import jax
import jax.numpy as jnp
from jax import lax
from jax.sharding import PartitionSpec as P

STEPS = 2


VELOCITIES = [
    (0, 0, 0),
    (1, 0, 0),
    (-1, 0, 0),
    (0, 1, 0),
    (0, -1, 0),
    (0, 0, 1),
    (0, 0, -1),
    (1, 1, 0),
    (-1, -1, 0),
    (1, -1, 0),
    (-1, 1, 0),
    (1, 0, 1),
    (-1, 0, -1),
    (1, 0, -1),
    (-1, 0, 1),
    (0, 1, 1),
    (0, -1, -1),
    (0, 1, -1),
    (0, -1, 1),
]
WEIGHTS = [1.0 / 3.0] + [1.0 / 18.0] * 6 + [1.0 / 36.0] * 12
OPPOSITE = [0, 2, 1, 4, 3, 6, 5, 8, 7, 10, 9, 12, 11, 14, 13, 16, 15, 18, 17]
TAU_BASE = 0.6
SMAG_COEF = 18.0 * 2.0**0.5 * 0.17**2


def from_partner(block, axis, stride):
    count = lax.axis_size(axis)
    route = []
    for low in range(count):
        high = low | 1 << stride
        if high != low and high < count:
            route += [(low, high), (high, low)]
    return lax.ppermute(block, axis, route)


def from_behind(block, axis, distance):
    devices = range(lax.axis_size(axis))
    route = [((i - distance) % len(devices), i) for i in devices]
    return lax.ppermute(block, axis, route)


def with_halo(shard, sides, width):
    for axis, dim in sides:
        peers, length = (lax.axis_size(axis), shard.shape[dim])
        up = [(i, (i + 1) % peers) for i in range(peers)]
        down = [(j, i) for i, j in up]
        last = lax.slice_in_dim(shard, length - width, length, axis=dim)
        leading = lax.slice_in_dim(shard, 0, width, axis=dim)
        before = lax.ppermute(last, axis, up)
        after = lax.ppermute(leading, axis, down)
        shard = jnp.concatenate([before, shard, after], axis=dim)
    return shard


def column(values, dim_count):
    return jnp.array(values, jnp.float32).reshape((19,) + (1,) * (dim_count - 1))


def collide(distribution):
    dim_count = distribution.ndim
    comp_x = column([v[0] for v in VELOCITIES], dim_count)
    comp_y = column([v[1] for v in VELOCITIES], dim_count)
    comp_z = column([v[2] for v in VELOCITIES], dim_count)
    weight = column(WEIGHTS, dim_count)
    density = jnp.sum(distribution, 0)
    vel_x = jnp.sum(comp_x * distribution, 0) / density
    vel_y = jnp.sum(comp_y * distribution, 0) / density
    vel_z = jnp.sum(comp_z * distribution, 0) / density
    project = comp_x * vel_x + comp_y * vel_y + comp_z * vel_z
    speed_sq = vel_x * vel_x + vel_y * vel_y + vel_z * vel_z
    equil = weight * density * (1.0 + 3.0 * project + 4.5 * project * project - 1.5 * speed_sq)
    noneq = distribution - equil
    stress_xx = jnp.sum(comp_x * comp_x * noneq, 0)
    stress_yy = jnp.sum(comp_y * comp_y * noneq, 0)
    stress_zz = jnp.sum(comp_z * comp_z * noneq, 0)
    stress_xy = jnp.sum(comp_x * comp_y * noneq, 0)
    stress_xz = jnp.sum(comp_x * comp_z * noneq, 0)
    stress_yz = jnp.sum(comp_y * comp_z * noneq, 0)
    strength = jnp.sqrt(
        stress_xx * stress_xx
        + stress_yy * stress_yy
        + stress_zz * stress_zz
        + 2.0 * (stress_xy * stress_xy + stress_xz * stress_xz + stress_yz * stress_yz)
    )
    relax_time = 0.5 * (TAU_BASE + jnp.sqrt(TAU_BASE * TAU_BASE + SMAG_COEF * strength / density))
    return distribution - noneq / relax_time


def table_rows(table, near_cols, near_rows):
    sel_x = (jnp.arange(table.shape[0], dtype=jnp.int32)[None, :] == near_cols[:, None]).astype(
        jnp.int32
    )
    partial_value = jnp.sum(sel_x[:, :, None, None] * table[None], axis=1)
    sel_y = (jnp.arange(table.shape[1], dtype=jnp.int32)[None, :] == near_rows[:, None]).astype(
        jnp.int32
    )
    return jnp.sum(sel_y[None, :, :, None] * partial_value[:, None], axis=2)


def holdings(live_self, move_self, live_other, move_other, pair_side):
    slot_count = live_self.shape[0]
    slot_ids = jnp.arange(slot_count, dtype=jnp.int32)
    rank_self = jnp.cumsum(live_self.astype(jnp.int32)) - 1
    rank_other = jnp.cumsum(live_other.astype(jnp.int32)) - 1
    usable = jnp.concatenate([live_self & jnp.logical_not(move_self), move_other])
    rank_new = jnp.cumsum(usable.astype(jnp.int32)) - 1
    slot_hit = usable[None, :] & (rank_new[None, :] == slot_ids[:, None])
    from_self = slot_hit[:, :slot_count, None] & (
        rank_self[None, :, None] == slot_ids[None, None, :]
    )
    from_other = slot_hit[:, slot_count:, None] & (
        rank_other[None, :, None] == slot_ids[None, None, :]
    )
    take_self = jnp.any(from_self, axis=1).astype(jnp.float32)
    take_other = jnp.any(from_other, axis=1).astype(jnp.float32)
    pair_sides = jnp.arange(2, dtype=jnp.int32)[None, :, None]
    placement = slot_hit[:, None, :slot_count] & (pair_sides == pair_side) | slot_hit[
        :, None, slot_count:
    ] & (pair_sides == 1 - pair_side)
    held_count = jnp.sum(usable.astype(jnp.int32))
    return (take_self, take_other, placement.astype(jnp.float32), held_count)


def select_rows(table, data):
    row_ids = jnp.sum(table * jnp.arange(table.shape[1], dtype=jnp.float32)[None, :], 1).astype(
        jnp.int32
    )
    found = jnp.sum(table, 1) > 0.5
    picked = jnp.take(data, row_ids, axis=0)
    return jnp.where(found.reshape((-1,) + (1,) * (data.ndim - 1)), picked, 0.0)


def cell_mask(live_near, block_edge):
    along_x = jnp.concatenate(
        [live_near[0:1], jnp.repeat(live_near[1:3], block_edge, axis=0), live_near[3:4]], 0
    )
    along_x = jnp.transpose(along_x, (0, 2, 1))
    return jnp.concatenate(
        [
            jnp.repeat(along_x[:, :, 0:1], block_edge, axis=2),
            jnp.repeat(along_x[:, :, 1:2], block_edge * block_edge, axis=2),
            jnp.repeat(along_x[:, :, 2:3], block_edge, axis=2),
        ],
        2,
    )


def collide_held(held_blocks, held_count):

    def relax_one(index, result):
        cube = lax.dynamic_index_in_dim(held_blocks, index, 0, keepdims=False)
        return lax.dynamic_update_index_in_dim(result, collide(cube), index, 0)

    return lax.fori_loop(0, held_count, relax_one, jnp.zeros_like(held_blocks))


def place_blocks(placement, blocks):
    slot_count, count_q, block_edge, plane = blocks.shape
    table = jnp.transpose(placement, (1, 2, 0)).reshape(2 * slot_count, slot_count)
    picked = select_rows(table, blocks).reshape(2, slot_count, count_q, block_edge, plane)
    placed = jnp.transpose(picked, (2, 0, 3, 1, 4))
    return placed.reshape(count_q, 2 * block_edge, slot_count, plane)


def extract(placement, read, block_edge):
    slot_count = placement.shape[0]
    plane = read.shape[3]
    split_view = read.reshape(19, 2, block_edge, slot_count, plane)
    split_view = jnp.transpose(split_view, (1, 3, 0, 2, 4)).reshape(
        2 * slot_count, 19, block_edge, plane
    )
    return select_rows(placement.reshape(slot_count, 2 * slot_count), split_view)


def partner(relaxed):
    return from_partner(relaxed, "bx", 0)


def ghosts(region, block_edge):
    low_side = from_behind(region[:, -1:], "bx", 2)
    high_side = from_behind(region[:, :1], "bx", -2)
    widened = jnp.concatenate([low_side, region, high_side], 1)
    return with_halo(widened, (("by", 3),), block_edge)


def wrap_z(values, step_z, z_pos, block_edge):
    if step_z == 1:
        across = jnp.roll(jnp.roll(values, 1 - block_edge, -1), 1, -2)
        return jnp.where(z_pos == 0, across, jnp.roll(values, 1, -1))
    if step_z == -1:
        across = jnp.roll(jnp.roll(values, block_edge - 1, -1), -1, -2)
        return jnp.where(z_pos == block_edge - 1, across, jnp.roll(values, -1, -1))
    return values


def stream(extended, fluid_ext, block_edge):
    width_x = extended.shape[1] - 2
    plane = block_edge * block_edge
    z_pos = jnp.arange(plane, dtype=jnp.int32) % block_edge
    center = extended[:, 1:-1, :, block_edge : block_edge + plane]
    moved_list = []
    for index in range(19):
        step_x, step_y, step_z = VELOCITIES[index]
        start_y = (1 - step_y) * block_edge
        window = extended[index, 1 - step_x : 1 - step_x + width_x, :, start_y : start_y + plane]
        source = fluid_ext[1 - step_x : 1 - step_x + width_x, :, start_y : start_y + plane]
        window = wrap_z(window, step_z, z_pos, block_edge)
        source = wrap_z(source, step_z, z_pos, block_edge)
        moved_list.append(jnp.where(source, window, center[OPPOSITE[index]]))
    return jnp.stack(moved_list)


def shards(populations, live_blocks, moving):
    slot_count = populations.shape[2]
    block_edge = populations.shape[4]
    slot_data = populations.reshape(slot_count, 19, block_edge, block_edge * block_edge)
    here_x = lax.axis_index("bx")
    here_y = lax.axis_index("by")
    pair_side = here_x % 2
    first_x = here_x - pair_side
    near_cols = (first_x - 1 + jnp.arange(4, dtype=jnp.int32)) % lax.axis_size("bx")
    near_rows = (here_y - 1 + jnp.arange(3, dtype=jnp.int32)) % lax.axis_size("by")
    live_near = table_rows(live_blocks, near_cols, near_rows) > 0
    move_near = table_rows(moving, near_cols[1:3], near_rows[1:2]) > 0
    live_pair = live_near[1:3, 1]
    move_pair = move_near[:, 0]
    own_live = jnp.where(pair_side == 0, live_pair[0], live_pair[1])
    mate_live = jnp.where(pair_side == 0, live_pair[1], live_pair[0])
    own_move = jnp.where(pair_side == 0, move_pair[0], move_pair[1])
    mate_move = jnp.where(pair_side == 0, move_pair[1], move_pair[0])
    take_self, take_other, place_own, held_count = holdings(
        own_live, own_move, mate_live, mate_move, pair_side
    )
    unused_self, unused_other, place_mate, mate_count = holdings(
        mate_live, mate_move, own_live, own_move, 1 - pair_side
    )
    fluid_ext = cell_mask(live_near, block_edge)
    mate_start = from_partner(slot_data, "bx", 0)
    held_blocks = select_rows(take_self, slot_data) + select_rows(take_other, mate_start)
    for turn_index in range(STEPS):
        relaxed = collide_held(held_blocks, held_count)
        region = place_blocks(place_own, relaxed) + place_blocks(place_mate, partner(relaxed))
        extended = ghosts(region, block_edge)
        read = stream(extended, fluid_ext, block_edge)
        held_blocks = extract(place_own, read, block_edge)
    return held_blocks.reshape(1, 1, slot_count, 19, block_edge, block_edge * block_edge)


def solution(mesh):
    placed = (P("bx", "by", None, None, None, None), P(), P())
    return jax.shard_map(
        shards,
        mesh=mesh,
        in_specs=placed,
        out_specs=P("bx", "by", None, None, None, None),
        check_vma=False,
    )
```

profile of v0, /device:TPU:1, one launch (start us, length us, event | category | flops | bytes accessed | tf_op | source)
XLA Modules:
  0.0 218.5 jit_solution(9085467824027661313)
XLA Ops:
  0.0 16.0 %collective-permute-start = (f32[2,19,16,256]{3,2,1,0:T(8,128)}, f32[2,19,16,256]{3,2,1,0:T(8,128)S(1)}, u32[]{:S(2)}, u32[]{:S(2)}) collective-permute-start(f32[2,19,16,256]{3,2,1,0:T(8,128)} %bitcast.554), channel_id=1, source_target_pairs={{0,16},{16,0},{32,48},{48,32},{64,80},{80,64},{96,112},{112,96},{1... | collective-permute-start | bytes 1867784 | tf_op jit(solution)/shard_map/ppermute | solution.py:43
  16.1 0.7 copy.424
  18.5 0.7 copy.426
  23.9 0.8 fusion.114
  25.8 1.7 gather_fusion
  30.5 0.7 fusion.179
  31.4 0.7 fusion.181
  33.8 0.7 fusion.197
  36.0 2.0 while.26
  38.0 1.9 collective-permute-start.1
  41.2 0.7 collective-permute-done.1
  43.1 0.7 fusion.216
  46.7 1.9 collective-permute-start.2
  48.6 7.3 %collective-permute-start.3 = (f32[19,1,2,256]{3,1,2,0:T(1,128)S(1)}, f32[19,1,2,256]{3,1,2,0:T(1,128)S(1)}, u32[]{:S(2)}, u32[]{:S(2)}) collective-permute-start(f32[19,1,2,256]{3,1,2,0:T(1,128)S(1)} %get-tuple-element.469), channel_id=1, source_target_pairs={{32,0},{48,16},{64,32},{80,48},{96,64},{112,80},{128,96},{144,112}... | collective-permute-start | bytes 116744 | tf_op jit(solution)/shard_map/ppermute | solution.py:49
  66.0 0.7 fusion.68
  66.8 0.7 slice.1531
  69.5 0.7 slice_bitcast_fusion.16
  73.8 2.1 collective-permute-start.4
  75.8 1.0 copy.438
  76.9 9.5 %collective-permute-start.5 = (f32[19,34,2,16]{1,3,2,0:T(8,128)}, f32[19,34,2,16]{1,3,2,0:T(8,128)}, u32[]{:S(2)}, u32[]{:S(2)}) collective-permute-start(f32[19,34,2,16]{1,3,2,0:T(8,128)} %copy.438), channel_id=1, source_target_pairs={{1,0},{2,1},{3,2},{4,3},{5,4},{6,5},{7,6},{8,7},{9,8},{10,9},{11,1... | collective-permute-start | bytes 248072 | tf_op jit(solution)/shard_map/ppermute | solution.py:60
  86.4 0.8 fusion.149
  87.2 0.9 fusion.151
  89.5 0.7 fusion.79
  90.3 0.7 fusion.78
  91.8 17.1 %collective-permute-done.4 = f32[19,34,2,16]{1,3,2,0:T(8,128)} collective-permute-done((f32[19,34,2,16]{1,3,2,0:T(8,128)S(1)}, f32[19,34,2,16]{1,3,2,0:T(8,128)}, u32[]{:S(2)}, u32[]{:S(2)}) %collective-permute-start.4) | collective-permute-done | bytes 82720 | tf_op jit(solution)/shard_map/ppermute | solution.py:59
  108.9 1.3 copy.436
  110.2 1.3 copy.439
  125.2 2.0 gather_fusion.4
  127.9 2.0 while.27
  130.0 2.4 %collective-permute-start.6 = (f32[2,19,16,256]{3,2,1,0:T(8,128)S(1)}, f32[2,19,16,256]{3,2,1,0:T(8,128)S(1)}, u32[]{:S(2)}, u32[]{:S(2)}) collective-permute-start(f32[2,19,16,256]{3,2,1,0:T(8,128)S(1)} %get-tuple-element.205), channel_id=1, source_target_pairs={{0,16},{16,0},{32,48},{48,32},{64,80},{80,64},{96,112},{112,96},{1... | collective-permute-start | bytes 1867784 | tf_op jit(solution)/shard_map/ppermute | solution.py:43
  132.4 0.8 gather_fusion.5
  133.2 0.9 collective-permute-done.6
  134.0 0.7 gather_fusion.6
  135.2 0.7 fusion.214
  136.1 0.7 slice_bitcast_fusion.8
  138.9 1.9 collective-permute-start.7
  140.8 7.5 %collective-permute-start.8 = (f32[19,1,2,256]{3,1,2,0:T(1,128)S(1)}, f32[19,1,2,256]{3,1,2,0:T(1,128)S(1)}, u32[]{:S(2)}, u32[]{:S(2)}) collective-permute-start(f32[19,1,2,256]{3,1,2,0:T(1,128)S(1)} %get-tuple-element.446), channel_id=1, source_target_pairs={{32,0},{48,16},{64,32},{80,48},{96,64},{112,80},{128,96},{144,112}... | collective-permute-start | bytes 116744 | tf_op jit(solution)/shard_map/ppermute | solution.py:49
  158.4 0.7 fusion.58
  166.7 2.1 collective-permute-start.9
  168.8 1.0 copy.501
  169.8 9.4 %collective-permute-start.10 = (f32[19,34,2,16]{1,3,2,0:T(8,128)}, f32[19,34,2,16]{1,3,2,0:T(8,128)}, u32[]{:S(2)}, u32[]{:S(2)}) collective-permute-start(f32[19,34,2,16]{1,3,2,0:T(8,128)} %copy.501), channel_id=1, source_target_pairs={{1,0},{2,1},{3,2},{4,3},{5,4},{6,5},{7,6},{8,7},{9,8},{10,9},{11,1... | collective-permute-start | bytes 248072 | tf_op jit(solution)/shard_map/ppermute | solution.py:60
  179.2 0.9 fusion.125
  182.1 0.7 fusion.91
  183.5 15.7 %collective-permute-done.9 = f32[19,34,2,16]{1,3,2,0:T(8,128)} collective-permute-done((f32[19,34,2,16]{1,3,2,0:T(8,128)S(1)}, f32[19,34,2,16]{1,3,2,0:T(8,128)}, u32[]{:S(2)}, u32[]{:S(2)}) %collective-permute-start.9) | collective-permute-done | bytes 82720 | tf_op jit(solution)/shard_map/ppermute | solution.py:59
  199.2 1.3 copy.499
  200.5 1.3 copy.502
  215.5 2.0 gather_fusion.7
  217.5 1.0 fusion.54
  (662 shorter events, 87.3 us)
Async XLA Ops:
  0.0 34.6 %collective-permute-start = (f32[2,19,16,256]{3,2,1,0:T(8,128)}, f32[2,19,16,256]{3,2,1,0:T(8,128)S(1)}, u32[]{:S(2)}, u32[]{:S(2)}) collective-permute-start(f32[2,19,16,256]{3,2,1,0:T(8,128)} %bitcast.554), channel_id=1, source_target_pairs={{0,16},{16,0},{32,48},{48,32},{64,80},{80,64},{96,112},{112,96},{1... | collective-permute-start | bytes 1867784 | tf_op jit(solution)/shard_map/ppermute | solution.py:43
  27.7 12.9 %copy-start.156 = (s32[1024]{0:T(1024)}, s32[1024]{0:T(1024)S(1)}, u32[]{:S(2)}) copy-start(s32[1024]{0:T(1024)S(1)} %pad_clamp_fusion.2) | copy-start | bytes 12292
  27.8 14.2 %copy-start.157 = (s32[1024]{0:T(1024)}, s32[1024]{0:T(1024)S(1)}, u32[]{:S(2)}) copy-start(s32[1024]{0:T(1024)S(1)} %pad_clamp_fusion.1) | copy-start | bytes 12292
  27.9 14.7 %copy-start.162 = (pred[4]{0:T(512)(128)(4,1)}, pred[4]{0:T(512)(128)(4,1)S(1)}, u32[]{:S(2)}) copy-start(pred[4]{0:T(512)(128)(4,1)S(1)} %gt.63) | copy-start | bytes 16
  28.0 14.6 %copy-start.164 = (pred[4]{0:T(512)(128)(4,1)}, pred[4]{0:T(512)(128)(4,1)S(1)}, u32[]{:S(2)}) copy-start(pred[4]{0:T(512)(128)(4,1)S(1)} %gt.67) | copy-start | bytes 16
  28.0 38.0 %copy-start.151 = (pred[32,2,1]{0,1,2:T(4,128)(4,1)}, pred[32,2,1]{0,1,2:T(4,128)(4,1)S(1)}, u32[]{:S(2)}) copy-start(pred[32,2,1]{0,1,2:T(4,128)(4,1)S(1)} %copy.601) | copy-start | bytes 196
  28.1 61.3 %copy-start.51 = (pred[1,32,2,1]{3,1,2,0:T(8,128)(4,1)}, pred[1,32,2,1]{3,1,2,0:T(8,128)(4,1)S(1)}, u32[]{:S(2)}) copy-start(pred[1,32,2,1]{3,1,2,0:T(8,128)(4,1)S(1)} %concatenate.1300) | copy-start | bytes 196
  30.3 35.7 %copy-start.148 = (pred[32,2]{0,1:T(4,128)(4,1)}, pred[32,2]{0,1:T(4,128)(4,1)S(1)}, u32[]{:S(2)}) copy-start(pred[32,2]{0,1:T(4,128)(4,1)S(1)} %get-tuple-element.595) | copy-start | bytes 196
  38.0 3.9 %collective-permute-start.1 = (f32[2,19,16,256]{3,2,1,0:T(8,128)S(1)}, f32[2,19,16,256]{3,2,1,0:T(8,128)S(1)}, u32[]{:S(2)}, u32[]{:S(2)}) collective-permute-start(f32[2,19,16,256]{3,2,1,0:T(8,128)S(1)} %get-tuple-element.204), channel_id=1, source_target_pairs={{0,16},{16,0},{32,48},{48,32},{64,80},{80,64},{96,112},{112,96},{1... | collective-permute-start | bytes 1867784 | tf_op jit(solution)/shard_map/ppermute | solution.py:43
  46.7 19.3 %collective-permute-start.2 = (f32[19,1,2,256]{3,1,2,0:T(1,128)S(1)}, f32[19,1,2,256]{3,1,2,0:T(1,128)S(1)}, u32[]{:S(2)}, u32[]{:S(2)}) collective-permute-start(f32[19,1,2,256]{3,1,2,0:T(1,128)S(1)} %get-tuple-element.470), channel_id=1, source_target_pairs={{992,0},{1008,16},{0,32},{16,48},{32,64},{48,80},{64,96},{80,112},... | collective-permute-start | bytes 116744 | tf_op jit(solution)/shard_map/ppermute | solution.py:49
  48.6 17.4 %collective-permute-start.3 = (f32[19,1,2,256]{3,1,2,0:T(1,128)S(1)}, f32[19,1,2,256]{3,1,2,0:T(1,128)S(1)}, u32[]{:S(2)}, u32[]{:S(2)}) collective-permute-start(f32[19,1,2,256]{3,1,2,0:T(1,128)S(1)} %get-tuple-element.469), channel_id=1, source_target_pairs={{32,0},{48,16},{64,32},{80,48},{96,64},{112,80},{128,96},{144,112}... | collective-permute-start | bytes 116744 | tf_op jit(solution)/shard_map/ppermute | solution.py:49
  73.6 14.5 %copy-start.37 = (f32[1,32,2,256]{3,1,2,0:T(8,128)S(1)}, f32[1,32,2,256]{3,1,2,0:T(8,128)}, u32[]{:S(2)}) copy-start(f32[1,32,2,256]{3,1,2,0:T(8,128)} %get-tuple-element.467) | copy-start | bytes 196612
  73.6 15.1 %copy-start.36 = (f32[1,32,2,256]{3,1,2,0:T(8,128)S(1)}, f32[1,32,2,256]{3,1,2,0:T(8,128)}, u32[]{:S(2)}) copy-start(f32[1,32,2,256]{3,1,2,0:T(8,128)} %get-tuple-element.422) | copy-start | bytes 196612
  73.6 15.7 %copy-start.149 = (pred[32,2]{0,1:T(4,128)(4,1)S(1)}, pred[32,2]{0,1:T(4,128)(4,1)}, u32[]{:S(2)}) copy-start(pred[32,2]{0,1:T(4,128)(4,1)} %copy-done.148) | copy-start | bytes 196
  73.6 15.8 %copy-start.46 = (f32[1,2,16,2,256]{4,2,1,3,0:T(8,128)S(1)}, f32[1,2,16,2,256]{4,2,1,3,0:T(8,128)}, u32[]{:S(2)}) copy-start(f32[1,2,16,2,256]{4,2,1,3,0:T(8,128)} %copy.458) | copy-start | bytes 196612
  73.7 15.8 %copy-start.49 = (f32[1,32,2,255]{3,1,2,0:T(8,128)S(1)}, f32[1,32,2,255]{3,1,2,0:T(8,128)}, u32[]{:S(2)}) copy-start(f32[1,32,2,255]{3,1,2,0:T(8,128)} %slice_bitcast_fusion.16) | copy-start | bytes 195844
  73.7 15.8 %copy-start.86 = (f32[1,32,2,1]{3,1,2,0:T(8,128)S(1)}, f32[1,32,2,1]{3,1,2,0:T(8,128)}, u32[]{:S(2)}) copy-start(f32[1,32,2,1]{3,1,2,0:T(8,128)} %slice_bitcast_fusion.36) | copy-start | bytes 772
  73.7 15.8 %copy-start.119 = (pred[1,32,1,256]{3,1,2,0:T(8,128)(4,1)S(1)}, pred[1,32,1,256]{3,1,2,0:T(8,128)(4,1)}, u32[]{:S(2)}) copy-start(pred[1,32,1,256]{3,1,2,0:T(8,128)(4,1)} %get-tuple-element.529) | copy-start | bytes 24580
  73.7 15.8 %copy-start.121 = (pred[1,32,1,256]{3,1,2,0:T(8,128)(4,1)S(1)}, pred[1,32,1,256]{3,1,2,0:T(8,128)(4,1)}, u32[]{:S(2)}) copy-start(pred[1,32,1,256]{3,1,2,0:T(8,128)(4,1)} %get-tuple-element.530) | copy-start | bytes 24580
  73.7 15.8 %copy-start.142 = (pred[256]{0:T(512)(128)(4,1)S(1)}, pred[256]{0:T(512)(128)(4,1)}, u32[]{:S(2)}) copy-start(pred[256]{0:T(512)(128)(4,1)} %broadcast_compare_fusion.2) | copy-start | bytes 772
  73.7 16.5 %copy-start.152 = (pred[32,2,1]{0,1,2:T(4,128)(4,1)S(1)}, pred[32,2,1]{0,1,2:T(4,128)(4,1)}, u32[]{:S(2)}) copy-start(pred[32,2,1]{0,1,2:T(4,128)(4,1)} %copy-done.151) | copy-start | bytes 196
  73.7 16.6 %copy-start.45 = (f32[1,2,16,2,256]{4,2,1,3,0:T(8,128)S(1)}, f32[1,2,16,2,256]{4,2,1,3,0:T(8,128)}, u32[]{:S(2)}) copy-start(f32[1,2,16,2,256]{4,2,1,3,0:T(8,128)} %copy.455) | copy-start | bytes 196612
  73.7 16.6 %copy-start.48 = (f32[1,32,2,255]{3,1,2,0:T(8,128)S(1)}, f32[1,32,2,255]{3,1,2,0:T(8,128)}, u32[]{:S(2)}) copy-start(f32[1,32,2,255]{3,1,2,0:T(8,128)} %slice_bitcast_fusion.17) | copy-start | bytes 195844
  73.7 16.6 %copy-start.85 = (f32[1,32,2,1]{3,1,2,0:T(8,128)S(1)}, f32[1,32,2,1]{3,1,2,0:T(8,128)}, u32[]{:S(2)}) copy-start(f32[1,32,2,1]{3,1,2,0:T(8,128)} %slice_bitcast_fusion.37) | copy-start | bytes 772
  73.7 16.6 %copy-start.123 = (pred[1,32,1,256]{3,1,2,0:T(8,128)(4,1)S(1)}, pred[1,32,1,256]{3,1,2,0:T(8,128)(4,1)}, u32[]{:S(2)}) copy-start(pred[1,32,1,256]{3,1,2,0:T(8,128)(4,1)} %get-tuple-element.533) | copy-start | bytes 24580
  73.8 16.6 %copy-start.125 = (pred[1,32,1,256]{3,1,2,0:T(8,128)(4,1)S(1)}, pred[1,32,1,256]{3,1,2,0:T(8,128)(4,1)}, u32[]{:S(2)}) copy-start(pred[1,32,1,256]{3,1,2,0:T(8,128)(4,1)} %get-tuple-element.534) | copy-start | bytes 24580
  73.8 16.6 %copy-start.145 = (pred[256]{0:T(512)(128)(4,1)S(1)}, pred[256]{0:T(512)(128)(4,1)}, u32[]{:S(2)}) copy-start(pred[256]{0:T(512)(128)(4,1)} %broadcast_compare_fusion.1) | copy-start | bytes 772
  73.8 17.3 %copy-start.38 = (f32[32,2,241]{2,0,1:T(8,128)S(1)}, f32[32,2,241]{2,0,1:T(8,128)}, u32[]{:S(2)}) copy-start(f32[32,2,241]{2,0,1:T(8,128)} %slice.1531) | copy-start | bytes 185092
  73.8 35.1 %collective-permute-start.4 = (f32[19,34,2,16]{1,3,2,0:T(8,128)S(1)}, f32[19,34,2,16]{1,3,2,0:T(8,128)}, u32[]{:S(2)}, u32[]{:S(2)}) collective-permute-start(f32[19,34,2,16]{1,3,2,0:T(8,128)S(1)} %copy.435), channel_id=1, source_target_pairs={{0,1},{1,2},{2,3},{3,4},{4,5},{5,6},{6,7},{7,8},{8,9},{9,10},{10,1... | collective-permute-start | bytes 248072 | tf_op jit(solution)/shard_map/ppermute | solution.py:59
  76.9 33.3 %collective-permute-start.5 = (f32[19,34,2,16]{1,3,2,0:T(8,128)}, f32[19,34,2,16]{1,3,2,0:T(8,128)}, u32[]{:S(2)}, u32[]{:S(2)}) collective-permute-start(f32[19,34,2,16]{1,3,2,0:T(8,128)} %copy.438), channel_id=1, source_target_pairs={{1,0},{2,1},{3,2},{4,3},{5,4},{6,5},{7,6},{8,7},{9,8},{10,9},{11,1... | collective-permute-start | bytes 248072 | tf_op jit(solution)/shard_map/ppermute | solution.py:60
  130.0 4.1 %collective-permute-start.6 = (f32[2,19,16,256]{3,2,1,0:T(8,128)S(1)}, f32[2,19,16,256]{3,2,1,0:T(8,128)S(1)}, u32[]{:S(2)}, u32[]{:S(2)}) collective-permute-start(f32[2,19,16,256]{3,2,1,0:T(8,128)S(1)} %get-tuple-element.205), channel_id=1, source_target_pairs={{0,16},{16,0},{32,48},{48,32},{64,80},{80,64},{96,112},{112,96},{1... | collective-permute-start | bytes 1867784 | tf_op jit(solution)/shard_map/ppermute | solution.py:43
  138.9 19.6 %copy-start.150 = (pred[32,2]{0,1:T(4,128)(4,1)S(1)}, pred[32,2]{0,1:T(4,128)(4,1)}, u32[]{:S(2)}) copy-start(pred[32,2]{0,1:T(4,128)(4,1)} %copy-done.148) | copy-start | bytes 196
  138.9 19.6 %copy-start.153 = (pred[32,2,1]{0,1,2:T(4,128)(4,1)S(1)}, pred[32,2,1]{0,1,2:T(4,128)(4,1)}, u32[]{:S(2)}) copy-start(pred[32,2,1]{0,1,2:T(4,128)(4,1)} %copy-done.151) | copy-start | bytes 196
  138.9 19.5 %collective-permute-start.7 = (f32[19,1,2,256]{3,1,2,0:T(1,128)S(1)}, f32[19,1,2,256]{3,1,2,0:T(1,128)S(1)}, u32[]{:S(2)}, u32[]{:S(2)}) collective-permute-start(f32[19,1,2,256]{3,1,2,0:T(1,128)S(1)} %get-tuple-element.447), channel_id=1, source_target_pairs={{992,0},{1008,16},{0,32},{16,48},{32,64},{48,80},{64,96},{80,112},... | collective-permute-start | bytes 116744 | tf_op jit(solution)/shard_map/ppermute | solution.py:49
  140.8 17.6 %collective-permute-start.8 = (f32[19,1,2,256]{3,1,2,0:T(1,128)S(1)}, f32[19,1,2,256]{3,1,2,0:T(1,128)S(1)}, u32[]{:S(2)}, u32[]{:S(2)}) collective-permute-start(f32[19,1,2,256]{3,1,2,0:T(1,128)S(1)} %get-tuple-element.446), channel_id=1, source_target_pairs={{32,0},{48,16},{64,32},{80,48},{96,64},{112,80},{128,96},{144,112}... | collective-permute-start | bytes 116744 | tf_op jit(solution)/shard_map/ppermute | solution.py:49
  166.3 15.7 %copy-start.53 = (pred[1,32,2,1]{3,1,2,0:T(8,128)(4,1)S(1)}, pred[1,32,2,1]{3,1,2,0:T(8,128)(4,1)}, u32[]{:S(2)}) copy-start(pred[1,32,2,1]{3,1,2,0:T(8,128)(4,1)} %copy-done.51) | copy-start | bytes 196
  166.3 15.7 %copy-start.147 = (pred[256]{0:T(512)(128)(4,1)S(1)}, pred[256]{0:T(512)(128)(4,1)}, u32[]{:S(2)}) copy-start(pred[256]{0:T(512)(128)(4,1)} %broadcast_compare_fusion.1) | copy-start | bytes 772
  166.6 13.4 %copy-start.83 = (f32[32,2,15]{2,0,1:T(8,128)S(1)}, f32[32,2,15]{2,0,1:T(8,128)}, u32[]{:S(2)}) copy-start(f32[32,2,15]{2,0,1:T(8,128)} %slice.1622) | copy-start | bytes 11524
  166.6 14.1 %copy-start.35 = (f32[1,32,2,256]{3,1,2,0:T(8,128)S(1)}, f32[1,32,2,256]{3,1,2,0:T(8,128)}, u32[]{:S(2)}) copy-start(f32[1,32,2,256]{3,1,2,0:T(8,128)} %get-tuple-element.444) | copy-start | bytes 196612
  166.6 14.8 %copy-start.34 = (f32[1,32,2,256]{3,1,2,0:T(8,128)S(1)}, f32[1,32,2,256]{3,1,2,0:T(8,128)}, u32[]{:S(2)}) copy-start(f32[1,32,2,256]{3,1,2,0:T(8,128)} %get-tuple-element.416) | copy-start | bytes 196612
  166.6 15.4 %copy-start.44 = (f32[1,2,16,2,256]{4,2,1,3,0:T(8,128)S(1)}, f32[1,2,16,2,256]{4,2,1,3,0:T(8,128)}, u32[]{:S(2)}) copy-start(f32[1,2,16,2,256]{4,2,1,3,0:T(8,128)} %copy.521) | copy-start | bytes 196612
  166.7 15.4 %copy-start.47 = (f32[1,32,2,255]{3,1,2,0:T(8,128)S(1)}, f32[1,32,2,255]{3,1,2,0:T(8,128)}, u32[]{:S(2)}) copy-start(f32[1,32,2,255]{3,1,2,0:T(8,128)} %slice_bitcast_fusion.4) | copy-start | bytes 195844
  166.7 15.4 %copy-start.84 = (f32[1,32,2,1]{3,1,2,0:T(8,128)S(1)}, f32[1,32,2,1]{3,1,2,0:T(8,128)}, u32[]{:S(2)}) copy-start(f32[1,32,2,1]{3,1,2,0:T(8,128)} %slice_bitcast_fusion.24) | copy-start | bytes 772
  166.7 15.4 %copy-start.128 = (pred[1,32,1,256]{3,1,2,0:T(8,128)(4,1)S(1)}, pred[1,32,1,256]{3,1,2,0:T(8,128)(4,1)}, u32[]{:S(2)}) copy-start(pred[1,32,1,256]{3,1,2,0:T(8,128)(4,1)} %get-tuple-element.527) | copy-start | bytes 24580
  166.7 15.4 %copy-start.130 = (pred[1,32,1,256]{3,1,2,0:T(8,128)(4,1)S(1)}, pred[1,32,1,256]{3,1,2,0:T(8,128)(4,1)}, u32[]{:S(2)}) copy-start(pred[1,32,1,256]{3,1,2,0:T(8,128)(4,1)} %get-tuple-element.528) | copy-start | bytes 24580
  166.7 16.1 %copy-start.39 = (f32[32,2,241]{2,0,1:T(8,128)S(1)}, f32[32,2,241]{2,0,1:T(8,128)}, u32[]{:S(2)}) copy-start(f32[32,2,241]{2,0,1:T(8,128)} %slice.1615) | copy-start | bytes 185092
  166.7 32.5 %collective-permute-start.9 = (f32[19,34,2,16]{1,3,2,0:T(8,128)S(1)}, f32[19,34,2,16]{1,3,2,0:T(8,128)}, u32[]{:S(2)}, u32[]{:S(2)}) collective-permute-start(f32[19,34,2,16]{1,3,2,0:T(8,128)S(1)} %copy.498), channel_id=1, source_target_pairs={{0,1},{1,2},{2,3},{3,4},{4,5},{5,6},{6,7},{7,8},{8,9},{9,10},{10,1... | collective-permute-start | bytes 248072 | tf_op jit(solution)/shard_map/ppermute | solution.py:59
  169.8 30.7 %collective-permute-start.10 = (f32[19,34,2,16]{1,3,2,0:T(8,128)}, f32[19,34,2,16]{1,3,2,0:T(8,128)}, u32[]{:S(2)}, u32[]{:S(2)}) collective-permute-start(f32[19,34,2,16]{1,3,2,0:T(8,128)} %copy.501), channel_id=1, source_target_pairs={{1,0},{2,1},{3,2},{4,3},{5,4},{6,5},{7,6},{8,7},{9,8},{10,9},{11,1... | collective-permute-start | bytes 248072 | tf_op jit(solution)/shard_map/ppermute | solution.py:60
  (133 other events, 329.9 us)
where the time goes:
time: 223 us; the launch traced here: 218 us
  local copies, waits for them, and re-layouts  86.8 us (39%)
  starting transfers between devices  61.9 us (28%)
  waiting for transfers between devices  34.4 us (15%)
  other arithmetic  30.1 us (13%)
  between operations  2.9 us (1%)
  loops' own time  2.38 us (1%)
    ppermute x2, waiting for transfers between devices, with_halo(): before = lax.ppermute(last, axis, up)  32.8 us
    unnamed x381, local copies, waits for them, and re-layouts  24.6 us
    ppermute x3, starting transfers between devices, from_partner(): return lax.ppermute(block, axis, route)  20.3 us
    slice x36, local copies, waits for them, and re-layouts, stream(): moved_list.append(jnp.where(source, window, center[OPPOSITE[index]]))  18.9 us
    ppermute x2, starting transfers between devices, with_halo(): after = lax.ppermute(leading, axis, down)  18.9 us
    ppermute x4, starting transfers between devices, from_behind(): return lax.ppermute(block, axis, route)  18.6 us
    gather x8, local copies, waits for them, and re-layouts, select_rows(): picked = jnp.take(data, row_ids, axis=0)  9.01 us
    concatenate x23, local copies, waits for them, and re-layouts, wrap_z(): return jnp.where(z_pos == 0, across, jnp.roll(values, 1, -1))  8.95 us
  transfers between devices with their start and end apart: 11, of which 4 were waited for; matrix products, arithmetic and copies ran while one was open for 25% of the time, Pallas kernels for 0%

commit v1 on v0

v1 whole, which is shorter than its diff:
```python
import functools

import jax
import jax.numpy as jnp
from jax import lax
from jax.experimental import pallas as pl
from jax.experimental.pallas import tpu as pltpu
from jax.sharding import PartitionSpec as P

MESH = pl.DeviceIdType.MESH
VELOCITIES = [
    (0, 0, 0), (1, 0, 0), (-1, 0, 0), (0, 1, 0), (0, -1, 0), (0, 0, 1), (0, 0, -1),
    (1, 1, 0), (-1, -1, 0), (1, -1, 0), (-1, 1, 0), (1, 0, 1), (-1, 0, -1),
    (1, 0, -1), (-1, 0, 1), (0, 1, 1), (0, -1, -1), (0, 1, -1), (0, -1, 1),
]
OPPOSITE = [0, 2, 1, 4, 3, 6, 5, 8, 7, 10, 9, 12, 11, 14, 13, 16, 15, 18, 17]
SMAG_COEF = 18.0 * 2.0**0.5 * 0.17**2
SOLID = -1e30
SOLID_TEST = -1e29
RING_Y = ([3, 7, 10, 15, 17], [4, 8, 9, 16, 18])
F32 = jnp.float32


def collide(f):
    sums, diffs = {}, {}
    for i in range(1, 19, 2):
        sums[i] = f[i] + f[i + 1]
        diffs[i] = f[i] - f[i + 1]
    side_xy = sums[7] + sums[9]
    side_xz = sums[11] + sums[13]
    side_yz = sums[15] + sums[17]
    density = f[0] + (sums[1] + sums[3] + sums[5]) + (side_xy + side_xz + side_yz)
    mom_x = diffs[1] + (diffs[7] + diffs[9]) + (diffs[11] + diffs[13])
    mom_y = diffs[3] + (diffs[7] - diffs[9]) + (diffs[15] + diffs[17])
    mom_z = diffs[5] + (diffs[11] - diffs[13]) + (diffs[15] - diffs[17])
    inverse = 1.0 / density
    vel_x, vel_y, vel_z = mom_x * inverse, mom_y * inverse, mom_z * inverse
    third = density * (1.0 / 3.0)
    p_xx = sums[1] + side_xy + side_xz - third - mom_x * vel_x
    p_yy = sums[3] + side_xy + side_yz - third - mom_y * vel_y
    p_zz = sums[5] + side_xz + side_yz - third - mom_z * vel_z
    p_xy = sums[7] - sums[9] - mom_x * vel_y
    p_xz = sums[11] - sums[13] - mom_x * vel_z
    p_yz = sums[15] - sums[17] - mom_y * vel_z
    strength = jnp.sqrt(
        p_xx * p_xx + p_yy * p_yy + p_zz * p_zz + 2.0 * (p_xy * p_xy + p_xz * p_xz + p_yz * p_yz)
    )
    omega = 2.0 / (0.6 + jnp.sqrt(0.36 + SMAG_COEF * strength * inverse))
    keep = 1.0 - omega
    gain = omega * density
    speed = vel_x * vel_x + vel_y * vel_y + vel_z * vel_z
    base = 1.0 - 1.5 * speed
    edge, corner = gain * (1.0 / 18.0), gain * (1.0 / 36.0)
    base_edge, base_corner = edge * base, corner * base
    result = [None] * 19
    result[0] = f[0] * keep + (gain * (1.0 / 3.0)) * base
    along = {
        1: vel_x, 3: vel_y, 5: vel_z,
        7: vel_x + vel_y, 9: vel_x - vel_y, 11: vel_x + vel_z,
        13: vel_x - vel_z, 15: vel_y + vel_z, 17: vel_y - vel_z,
    }
    for i in range(1, 19, 2):
        weight, rest = (edge, base_edge) if i < 7 else (corner, base_corner)
        odd = 3.0 * weight * along[i]
        even = rest + (1.5 * odd) * along[i]
        result[i] = f[i] * keep + (even + odd)
        result[i + 1] = f[i + 1] * keep + (even - odd)
    return result


def lanes_of(shape):
    return lax.broadcasted_iota(jnp.int32, shape, len(shape) - 1)


def exchange(
    n_x, n_y, pop, live, move, col, xg, yg, cp, tab, fbuf, xs, ys, cs, in_sem, send_sem, recv_sem
):
    me_x, me_y = lax.axis_index("bx"), lax.axis_index("by")
    side = lax.rem(me_x, 2)
    mate = me_x + 1 - 2 * side
    outer = lax.rem(me_x + n_x - 1 + 2 * side, n_x)
    above = lax.rem(me_y + 1, n_y)
    below = lax.rem(me_y + n_y - 1, n_y)
    at_mate, at_outer = (mate, me_y), (outer, me_y)
    at_y = ((me_x, above), (me_x, below))

    barrier = pltpu.get_barrier_semaphore()
    for device in (at_mate, at_outer) + at_y:
        pl.semaphore_signal(barrier, inc=1, device_id=device, device_id_type=MESH)

    load_pop = pltpu.make_async_copy(pop, fbuf, in_sem.at[0])
    load_live = pltpu.make_async_copy(live.at[me_y], tab.at[0], in_sem.at[1])
    load_move = pltpu.make_async_copy(move.at[me_y], tab.at[1], in_sem.at[2])
    load_live.start()
    load_move.start()
    load_pop.start()
    load_live.wait()
    load_move.wait()
    load_pop.wait()

    row = tab[0]
    flags = jnp.sum(jnp.where(lanes_of(row.shape) == me_x, row, 0).astype(F32), axis=1, keepdims=True)
    first = jnp.broadcast_to(flags[0:1, :], (8, 128)) > 0.5
    second = jnp.broadcast_to(flags[1:2, :], (8, 128)) > 0.5

    for k in range(2):
        fluid = (first, second)[k]

        def relax(i, carry, k=k, fluid=fluid):
            tile, half = i // 2, i % 2
            rows = pl.ds(pl.multiple_of(half * 8, 8), 8)
            lanes = pl.ds(pl.multiple_of(tile * 128, 128), 128)
            f = [jnp.where(first, fbuf[k, q, rows, lanes], fbuf[1 - k, q, rows, lanes]) for q in range(19)]
            for q, value in enumerate(collide(f)):
                to = pl.ds(pl.multiple_of(q * 16 + half * 8, 8), 8)
                col[side, k, tile, to, :] = jnp.where(fluid, value, SOLID)
            return carry

        lax.fori_loop(0, 4, relax, 0)

    near, far = 15 * side, 1 + 13 * side
    for tile in range(2):
        for k in range(2):
            own = col.at[side, k, tile]
            xs[tile, k, 0:19, :] = own[pl.ds(near, 19, stride=16), :]
            xs[tile, k, 19:20, :] = own[pl.ds((2 - side) * 16 + far, 1), :]
            xs[tile, k, 20:24, :] = own[pl.ds((8 - side) * 16 + far, 4, stride=32), :]

    group = lanes_of((16, 128)) // 16

    def pack(k, carry):
        for way in range(2):
            tile, first_lane, second_lane = ((1, 112, 96), (0, 0, 16))[way]
            for g in range(3):
                packed = None
                for i in range(8):
                    p = 8 * g + i
                    q, lane = (p, first_lane) if p < 19 else (RING_Y[way][p - 19], second_lane)
                    value = col[side, k, tile, q * 16 : q * 16 + 16, :]
                    shift = (16 * i - lane) % 128
                    if shift:
                        value = pltpu.roll(value, shift, 1)
                    packed = value if packed is None else jnp.where(group == i, value, packed)
                ys[way, k, g] = packed
        return carry

    lax.fori_loop(0, 2, pack, 0)

    pl.semaphore_wait(barrier, 4)

    def send(index, source, target, device):
        copy = pltpu.make_async_remote_copy(
            src_ref=source,
            dst_ref=target,
            send_sem=send_sem.at[index],
            recv_sem=recv_sem.at[index],
            device_id=device,
            device_id_type=MESH,
        )
        copy.start()
        return copy

    to_outer = send(0, xs, xg.at[1 - side], at_outer)
    to_y = [send(1 + way, ys.at[way], yg.at[side, way], at_y[way]) for way in range(2)]
    whole = send(3, col.at[side], col.at[side], at_mate)

    to_outer.wait_recv()
    quarter = lanes_of((8, 128)) // 32
    for way in range(2):
        for k in range(2):
            packed = None
            for g in range(3):
                value = xg[side, 1 - way, k, 8 * g : 8 * g + 8, :]
                shift = (32 * g - (96, 0)[way]) % 128
                if shift:
                    value = pltpu.roll(value, shift, 1)
                packed = value if packed is None else jnp.where(quarter == g, value, packed)
            cs[way, k] = packed
    corners = [send(4 + way, cs.at[way], cp.at[side, way], at_y[way]) for way in range(2)]
    relays = [send(6, xg.at[side], xg.at[side], at_mate)]
    for way in range(2):
        to_y[way].wait_recv()
        relays.append(send(7 + way, yg.at[side, way], yg.at[side, way], at_mate))
    for way in range(2):
        corners[way].wait_recv()
        relays.append(send(9 + way, cp.at[side, way], cp.at[side, way], at_mate))
    whole.wait_recv()
    for copy in relays:
        copy.wait_recv()
    for copy in [to_outer, whole] + to_y + corners + relays:
        copy.wait_send()


def stream(source, q, row, tiles):
    _, step_y, step_z = VELOCITIES[q]
    need = sorted({(t - d) % 3 for t in tiles for d in ((0, step_y) if step_y else (0,))})
    data = [{t: source[k, t, pl.ds(row, 8), :] for t in need} for k in range(2)]
    lane = lanes_of((8, 128))

    def turn(value, shift):
        return pltpu.roll(value, shift % 128, 1) if shift % 128 else value

    if step_z:
        at_edge = lane % 16 == (0 if step_z == 1 else 15)
        moved = [
            {
                t: jnp.where(
                    at_edge,
                    turn(data[1 - k][t], 16 * step_y - 15 * step_z),
                    turn(data[k][t], 16 * step_y + step_z),
                )
                for t in need
            }
            for k in range(2)
        ]
    else:
        moved = [{t: turn(data[k][t], 16 * step_y) for t in need} for k in range(2)]
    if step_y:
        crossed = lane < 16 if step_y == 1 else lane >= 112
        moved = [
            {t: jnp.where(crossed, moved[k][(t - step_y) % 3], moved[k][t]) for t in tiles}
            for k in range(2)
        ]
    return moved


def advance(col, xg, yg, cp, tab, out, ext, nxt, ux, fs):
    me_x = lax.axis_index("bx")
    side = lax.rem(me_x, 2)
    mate = me_x + 1 - 2 * side

    def bit(table, device, k):
        row = tab[table]
        hit = (lanes_of(row.shape) == device) & (lax.broadcasted_iota(jnp.int32, row.shape, 0) == k)
        return jnp.sum(jnp.where(hit, row, 0).astype(F32))

    own_live = [bit(0, me_x, k) for k in range(2)]
    own_moving = [bit(1, me_x, k) for k in range(2)]
    arriving = [bit(1, mate, k) for k in range(2)]
    swap = (own_live[0] + own_live[1] < 0.5) & (arriving[0] + arriving[1] > 0.5)
    chosen = [
        jnp.where(swap, arriving[k], own_live[k] * (1.0 - own_moving[k])) > 0.5 for k in range(2)
    ]
    sc = jnp.where(swap, 1 - side, side)

    outer_near, outer_far = 7 + 17 * sc, 6 + 19 * sc
    inner_near, inner_far = 24 - 17 * sc, 25 - 19 * sc
    mate_near, mate_far = 15 * sc, 1 + 13 * sc
    lane8 = lanes_of((8, 128))

    def place_outer(k, tile, planes):
        ext[k, tile, pl.ds(outer_near, 19, stride=32), :] = planes[0:19, :]
        ext[k, tile, pl.ds((1 + sc) * 32 + outer_far, 1), :] = planes[19:20, :]
        ext[k, tile, pl.ds((7 + sc) * 32 + outer_far, 4, stride=64), :] = planes[20:24, :]

    for k in range(2):
        for tile in range(2):
            for q in range(19):
                ext[k, tile, q * 32 + 8 : q * 32 + 24, :] = col[sc, k, tile, q * 16 : q * 16 + 16, :]
            place_outer(k, tile, xg.at[sc, tile, k])
            ext[k, tile, pl.ds(inner_near, 19, stride=32), :] = col[
                1 - sc, k, tile, pl.ds(mate_near, 19, stride=16), :
            ]
            ext[k, tile, pl.ds(inner_far, 19, stride=32), :] = col[
                1 - sc, k, tile, pl.ds(mate_far, 19, stride=16), :
            ]
        for g in range(3):
            low = cp[sc, 0, k]
            high = cp[sc, 1, k]
            low = pltpu.roll(low, (96 - 32 * g) % 128, 1)
            high = pltpu.roll(high, (-32 * g) % 128, 1) if g else high
            ux[k, 8 * g : 8 * g + 8, :] = jnp.where(lane8 < 64, high, low)
        place_outer(k, 2, ux.at[k])

        for own in range(2):
            rows = 16 if own else 8
            lane = lanes_of((rows, 128))
            for q in range(19):
                parts = []
                for way in range(2):
                    near_lane, far_lane = ((112, 96), (0, 16))[way]

                    def unit(p, lane_to, way=way):
                        if own:
                            value = yg[sc, way, k, p // 8]
                        else:
                            value = yg[1 - sc, way, k, p // 8, pl.ds(pl.multiple_of(8 * sc, 8), 8), :]
                        shift = (lane_to - 16 * (p % 8)) % 128
                        return pltpu.roll(value, shift, 1) if shift else value

                    value = unit(q, near_lane)
                    if q in RING_Y[way]:
                        far = unit(19 + RING_Y[way].index(q), far_lane)
                        value = jnp.where(lane // 16 == near_lane // 16, value, far)
                    parts.append(value)
                value = jnp.where(lane < 64, parts[1], parts[0])
                if own:
                    ext[k, 2, q * 32 + 8 : q * 32 + 24, :] = value
                else:
                    ext[k, 2, pl.ds(pl.multiple_of(q * 32 + 24 - 24 * sc, 8), 8), :] = value

    def arrive(source, stride, base, q, row, tiles):
        moved = stream(source, q, q * stride + base + row - VELOCITIES[q][0], tiles)
        result = {}
        for k in range(2):
            for t in tiles:
                value = moved[k][t]
                if q:
                    back = source[k, t, pl.ds(OPPOSITE[q] * stride + base + row, 8), :]
                    value = jnp.where(value > SOLID_TEST, value, back)
                result[k, t] = value
        return result

    for chunk in range(3):
        for q in range(19):
            for (k, t), value in arrive(ext, 32, 7, q, 8 * chunk, (0, 1, 2)).items():
                fs[q, k, t] = value
        for k in range(2):
            for t in range(3):
                f = [fs[q, k, t] for q in range(19)]
                fluid = f[0] > SOLID_TEST
                for q, value in enumerate(collide(f)):
                    nxt[k, t, q * 24 + 8 * chunk : q * 24 + 8 * chunk + 8, :] = jnp.where(
                        fluid, value, SOLID
                    )

    zero = jnp.zeros((8, 128), F32)
    both = chosen[0] & chosen[1]
    for chunk in range(2):
        for q in range(19):
            values = arrive(nxt, 24, 1, q, 8 * chunk, (0, 1))
            for t in range(2):
                spot = (q, slice(8 * chunk, 8 * chunk + 8), slice(128 * t, 128 * t + 128))
                lower, upper = values[0, t], values[1, t]
                out[(0,) + spot] = jnp.where(chosen[0], lower, jnp.where(chosen[1], upper, zero))
                out[(1,) + spot] = jnp.where(both, upper, zero)


VMEM = pl.BlockSpec(memory_space=pltpu.VMEM)
HBM = pl.BlockSpec(memory_space=pltpu.HBM)


def shards(n_x, n_y, populations, live_blocks, moving):
    pop, live, move = (
        pltpu.with_memory_space_constraint(array, pltpu.HBM)
        for array in (
            populations.reshape(2, 19, 16, 256),
            jnp.transpose(live_blocks, (1, 2, 0)),
            jnp.transpose(moving, (1, 2, 0)),
        )
    )
    shapes = [(2, 2, 2, 304, 128), (2, 2, 2, 24, 128), (2, 2, 2, 3, 16, 128), (2, 2, 2, 8, 128)]
    parts = pl.pallas_call(
        functools.partial(exchange, n_x, n_y),
        out_shape=[jax.ShapeDtypeStruct(shape, F32) for shape in shapes]
        + [jax.ShapeDtypeStruct((2, 2, n_x), jnp.int32)],
        in_specs=[HBM] * 3,
        out_specs=[VMEM] * 5,
        scratch_shapes=[
            pltpu.VMEM((2, 19, 16, 256), F32),
            pltpu.VMEM((2, 2, 24, 128), F32),
            pltpu.VMEM((2, 2, 3, 16, 128), F32),
            pltpu.VMEM((2, 2, 8, 128), F32),
            pltpu.SemaphoreType.DMA((3,)),
            pltpu.SemaphoreType.DMA((11,)),
            pltpu.SemaphoreType.DMA((11,)),
        ],
        compiler_params=pltpu.CompilerParams(
            collective_id=0, has_side_effects=True, vmem_limit_bytes=8 << 20
        ),
        name="exchange",
    )(pop, live, move)
    result = pl.pallas_call(
        advance,
        out_shape=jax.ShapeDtypeStruct((2, 19, 16, 256), F32),
        in_specs=[VMEM] * 5,
        out_specs=VMEM,
        scratch_shapes=[
            pltpu.VMEM((2, 3, 19 * 32, 128), F32),
            pltpu.VMEM((2, 3, 19 * 24, 128), F32),
            pltpu.VMEM((2, 24, 128), F32),
            pltpu.VMEM((19, 2, 3, 8, 128), F32),
        ],
        compiler_params=pltpu.CompilerParams(vmem_limit_bytes=12 << 20),
        name="advance",
    )(*parts)
    return result.reshape(1, 1, 2, 19, 16, 256)


def solution(mesh):
    n_x, n_y = mesh.shape["bx"], mesh.shape["by"]
    placed = (P("bx", "by", None, None, None, None), P(), P())
    return jax.shard_map(
        functools.partial(shards, n_x, n_y),
        mesh=mesh,
        in_specs=placed,
        out_specs=P("bx", "by", None, None, None, None),
        check_vma=False,
    )
```

time: 223 us -> 35.9 us (0.16); the launches traced: 218 us -> 35.8 us
  local copies, waits for them, and re-layouts: 86.8 us -> 0 us
  starting transfers between devices: 61.9 us -> 0 us
  Pallas kernels: 0 us -> 35.8 us
  waiting for transfers between devices: 34.4 us -> 0 us
  other arithmetic: 30.1 us -> 0 us
  between operations: 2.9 us -> 0.01 us
  loops' own time: 2.38 us -> 0 us
    ppermute x11 -> x0, starting transfers between devices: 61.9 us -> none  [the longest x3 20.3 us: from_partner(): return lax.ppermute(block, axis, route)]
    pallas_call x0 -> x2, Pallas kernels: none -> 35.8 us  [the longest x1 33.2 us: shards(): pl.pallas_call(functools.partial(exchange, n_x, n_y), out_shape=[jax.Shap...]
    ppermute x11 -> x0, waiting for transfers between devices: 34.4 us -> none  [the longest x2 32.8 us: with_halo(): before = lax.ppermute(last, axis, up)]
    slice x94 -> x0, local copies, waits for them, and re-layouts: 29.8 us -> none  [the longest x36 18.9 us: stream(): moved_list.append(jnp.where(source, window, center[OPPOSITE[index]]))]
    unnamed x381 -> x0, local copies, waits for them, and re-layouts: 24.6 us -> none
    concatenate x45 -> x0, local copies, waits for them, and re-layouts: 15.5 us -> none  [the longest x23 8.95 us: wrap_z(): return jnp.where(z_pos == 0, across, jnp.roll(values, 1, -1))]
    concatenate x30 -> x0, other arithmetic: 13.3 us -> none  [the longest x13 6.97 us: wrap_z(): across = jnp.roll(jnp.roll(values, 1 - block_edge, -1), 1, -2)]
    gather x8 -> x0, local copies, waits for them, and re-layouts: 9.01 us -> none  [select_rows(): picked = jnp.take(data, row_ids, axis=0)]
  transfers between devices with their start and end apart: 11 -> 0, of which waited for: 4 -> 0; matrix products, arithmetic and copies ran while one was open for 25% -> 0% of each run, Pallas kernels for 0% -> 0%
where the time goes in v1:
time: 35.9 us; the launch traced here: 35.8 us
  Pallas kernels  35.8 us (100%)
    pallas_call x1, Pallas kernels, shards(): pl.pallas_call(functools.partial(exchange, n_x, n_y), out_shape=[jax.Shap...  33.2 us
    pallas_call x1, Pallas kernels, shards(): pl.pallas_call(advance, out_shape=jax.ShapeDtypeStruct((2, 19, 16, 256),...  2.54 us

profile of v1, /device:TPU:1, one launch (start us, length us, event | category | flops | bytes accessed | tf_op | source)
XLA Modules:
  0.0 35.8 jit_solution(14459920156559341999)
XLA Ops:
  0.0 33.2 %exchange.1 = (f32[2,2,2,304,128]{4,3,2,1,0:T(8,128)S(1)}, f32[2,2,2,24,128]{4,3,2,1,0:T(8,128)S(1)}, f32[2,2,2,3,16,128]{5,4,3,2,1,0:T(8,128)S(1)}, f32[2,2,2,8,128]{4,3,2,1,0:T(8,128)S(1)}, s32[2,2,64]{2,1,0:T(2,128)S(1)}) custom-call(f32[2,19,16,256]{3,2,1,0:T(8,128)} %bitcast.4, s32[16,2,64]{2,1,0:T(2,128)} %bitcast.5, s32[16,2,64]{2,1,0:T(2,128)} %bitcast.6), custom_call_target="tpu_custom_call" | custom-call | tf_op jit(solution)/shard_map/exchange/pallas_call | solution.py:353
  33.2 2.5 %advance.1 = f32[2,19,16,256]{3,2,1,0:T(8,128)} custom-call(f32[2,2,2,304,128]{4,3,2,1,0:T(8,128)S(1)} %get-tuple-element.10.col, f32[2,2,2,24,128]{4,3,2,1,0:T(8,128)S(1)} %get-tuple-element.11.xg, f32[2,2,2,3,16,128]{5,4,3,2,1,0:T(8,128)S(1)} %get-tuple-element.12.yg, f32[2,2,2,8,128]{4,3,2,1,0:T(8,128)S(1)} %get-tuple-element.13.cp, ...), custom_call_target="tpu_custom_call" | custom-call | tf_op jit(solution)/shard_map/advance/pallas_call | solution.py:373

commit v2 on v1

--- a/solution.py
+++ b/solution.py
@@ -73,83 +73,34 @@
 
 
 def exchange(
-    n_x, n_y, pop, live, move, col, xg, yg, cp, tab, fbuf, xs, ys, cs, in_sem, send_sem, recv_sem
+    n_x, n_y, pop, live, move, col, xg, yg, cp, tab,
+    fbuf, xs, ys, cs, in_sem, send_sem, recv_sem, ready,
 ):
     me_x, me_y = lax.axis_index("bx"), lax.axis_index("by")
     side = lax.rem(me_x, 2)
-    mate = me_x + 1 - 2 * side
-    outer = lax.rem(me_x + n_x - 1 + 2 * side, n_x)
-    above = lax.rem(me_y + 1, n_y)
-    below = lax.rem(me_y + n_y - 1, n_y)
-    at_mate, at_outer = (mate, me_y), (outer, me_y)
-    at_y = ((me_x, above), (me_x, below))
-
+    base = me_x - side
+    at_mate = (base + 1 - side, me_y)
+    at_x = (
+        (lax.rem(base + n_x - 1, n_x), me_y),
+        (lax.rem(base + 3, n_x), me_y),
+    )
+    at_y = ((base + 1, lax.rem(me_y + 1, n_y)), (base + 1, lax.rem(me_y + n_y - 1, n_y)))
     barrier = pltpu.get_barrier_semaphore()
-    for device in (at_mate, at_outer) + at_y:
-        pl.semaphore_signal(barrier, inc=1, device_id=device, device_id_type=MESH)
-
-    load_pop = pltpu.make_async_copy(pop, fbuf, in_sem.at[0])
+
+    @pl.when(side == 1)
+    def _():
+        for device in at_x + at_y + (at_mate,):
+            pl.semaphore_signal(barrier, inc=1, device_id=device, device_id_type=MESH)
+
+    load_pop = pltpu.make_async_copy(pop, fbuf.at[side], in_sem.at[0])
     load_live = pltpu.make_async_copy(live.at[me_y], tab.at[0], in_sem.at[1])
     load_move = pltpu.make_async_copy(move.at[me_y], tab.at[1], in_sem.at[2])
+    load_pop.start()
     load_live.start()
     load_move.start()
-    load_pop.start()
-    load_live.wait()
-    load_move.wait()
-    load_pop.wait()
-
-    row = tab[0]
-    flags = jnp.sum(jnp.where(lanes_of(row.shape) == me_x, row, 0).astype(F32), axis=1, keepdims=True)
-    first = jnp.broadcast_to(flags[0:1, :], (8, 128)) > 0.5
-    second = jnp.broadcast_to(flags[1:2, :], (8, 128)) > 0.5
-
-    for k in range(2):
-        fluid = (first, second)[k]
-
-        def relax(i, carry, k=k, fluid=fluid):
-            tile, half = i // 2, i % 2
-            rows = pl.ds(pl.multiple_of(half * 8, 8), 8)
-            lanes = pl.ds(pl.multiple_of(tile * 128, 128), 128)
-            f = [jnp.where(first, fbuf[k, q, rows, lanes], fbuf[1 - k, q, rows, lanes]) for q in range(19)]
-            for q, value in enumerate(collide(f)):
-                to = pl.ds(pl.multiple_of(q * 16 + half * 8, 8), 8)
-                col[side, k, tile, to, :] = jnp.where(fluid, value, SOLID)
-            return carry
-
-        lax.fori_loop(0, 4, relax, 0)
-
-    near, far = 15 * side, 1 + 13 * side
-    for tile in range(2):
-        for k in range(2):
-            own = col.at[side, k, tile]
-            xs[tile, k, 0:19, :] = own[pl.ds(near, 19, stride=16), :]
-            xs[tile, k, 19:20, :] = own[pl.ds((2 - side) * 16 + far, 1), :]
-            xs[tile, k, 20:24, :] = own[pl.ds((8 - side) * 16 + far, 4, stride=32), :]
-
-    group = lanes_of((16, 128)) // 16
-
-    def pack(k, carry):
-        for way in range(2):
-            tile, first_lane, second_lane = ((1, 112, 96), (0, 0, 16))[way]
-            for g in range(3):
-                packed = None
-                for i in range(8):
-                    p = 8 * g + i
-                    q, lane = (p, first_lane) if p < 19 else (RING_Y[way][p - 19], second_lane)
-                    value = col[side, k, tile, q * 16 : q * 16 + 16, :]
-                    shift = (16 * i - lane) % 128
-                    if shift:
-                        value = pltpu.roll(value, shift, 1)
-                    packed = value if packed is None else jnp.where(group == i, value, packed)
-                ys[way, k, g] = packed
-        return carry
-
-    lax.fori_loop(0, 2, pack, 0)
-
-    pl.semaphore_wait(barrier, 4)
-
-    def send(index, source, target, device):
-        copy = pltpu.make_async_remote_copy(
+
+    def link(index, source, target, device):
+        return pltpu.make_async_remote_copy(
             src_ref=source,
             dst_ref=target,
             send_sem=send_sem.at[index],
@@ -157,38 +108,130 @@
             device_id=device,
             device_id_type=MESH,
         )
-        copy.start()
-        return copy
-
-    to_outer = send(0, xs, xg.at[1 - side], at_outer)
-    to_y = [send(1 + way, ys.at[way], yg.at[side, way], at_y[way]) for way in range(2)]
-    whole = send(3, col.at[side], col.at[side], at_mate)
-
-    to_outer.wait_recv()
-    quarter = lanes_of((8, 128)) // 32
-    for way in range(2):
+
+    raw = link(0, pop, fbuf.at[side], at_mate)
+
+    @pl.when(side == 0)
+    def _():
+        pl.semaphore_wait(barrier, 1)
+        pl.semaphore_signal(ready, inc=1, device_id=at_mate, device_id_type=MESH)
+        raw.start()
+
+    load_live.wait()
+    load_move.wait()
+    load_pop.wait()
+
+    def relax_column(c):
+        row = tab[0]
+        hit = lanes_of(row.shape) == base + c
+        flags = jnp.sum(jnp.where(hit, row, 0).astype(F32), axis=1, keepdims=True)
+        first = jnp.broadcast_to(flags[0:1, :], (8, 128)) > 0.5
+        second = jnp.broadcast_to(flags[1:2, :], (8, 128)) > 0.5
         for k in range(2):
-            packed = None
-            for g in range(3):
-                value = xg[side, 1 - way, k, 8 * g : 8 * g + 8, :]
-                shift = (32 * g - (96, 0)[way]) % 128
-                if shift:
-                    value = pltpu.roll(value, shift, 1)
-                packed = value if packed is None else jnp.where(quarter == g, value, packed)
-            cs[way, k] = packed
-    corners = [send(4 + way, cs.at[way], cp.at[side, way], at_y[way]) for way in range(2)]
-    relays = [send(6, xg.at[side], xg.at[side], at_mate)]
-    for way in range(2):
-        to_y[way].wait_recv()
-        relays.append(send(7 + way, yg.at[side, way], yg.at[side, way], at_mate))
-    for way in range(2):
-        corners[way].wait_recv()
-        relays.append(send(9 + way, cp.at[side, way], cp.at[side, way], at_mate))
-    whole.wait_recv()
-    for copy in relays:
-        copy.wait_recv()
-    for copy in [to_outer, whole] + to_y + corners + relays:
-        copy.wait_send()
+            fluid = (first, second)[k]
+
+            def relax(i, carry, k=k, fluid=fluid):
+                tile, half = i // 2, i % 2
+                rows = pl.ds(pl.multiple_of(half * 8, 8), 8)
+                lanes = pl.ds(pl.multiple_of(tile * 128, 128), 128)
+                f = [
+                    jnp.where(first, fbuf[c, k, q, rows, lanes], fbuf[c, 1 - k, q, rows, lanes])
+                    for q in range(19)
+                ]
+                for q, value in enumerate(collide(f)):
+                    to = pl.ds(pl.multiple_of(q * 16 + half * 8, 8), 8)
+                    col[c, k, tile, to, :] = jnp.where(fluid, value, SOLID)
+                return carry
+
+            lax.fori_loop(0, 4, relax, 0)
+
+    group = lanes_of((16, 128)) // 16
+
+    def pack_column(c):
+        near, far = 15 * c, 1 + 13 * c
+        for tile in range(2):
+            for k in range(2):
+                own = col.at[c, k, tile]
+                xs[c, tile, k, 0:19, :] = own[pl.ds(near, 19, stride=16), :]
+                xs[c, tile, k, 19:20, :] = own[pl.ds((2 - c) * 16 + far, 1), :]
+                xs[c, tile, k, 20:24, :] = own[pl.ds((8 - c) * 16 + far, 4, stride=32), :]
+
+        def pack(k, carry):
+            for way in range(2):
+                tile, first_lane, second_lane = ((1, 112, 96), (0, 0, 16))[way]
+                for g in range(3):
+                    packed = None
+                    for i in range(8):
+                        p = 8 * g + i
+                        q, lane = (p, first_lane) if p < 19 else (RING_Y[way][p - 19], second_lane)
+                        value = col[c, k, tile, q * 16 : q * 16 + 16, :]
+                        shift = (16 * i - lane) % 128
+                        if shift:
+                            value = pltpu.roll(value, shift, 1)
+                        packed = value if packed is None else jnp.where(group == i, value, packed)
+                    ys[way, c, k, g] = packed
+            return carry
+
+        lax.fori_loop(0, 2, pack, 0)
+
+    relax_column(side)
+
+    @pl.when(side == 1)
+    def _():
+        pack_column(1)
+        pl.semaphore_wait(ready, 1)
+        raw.start()
+
+    raw.wait_recv()
+    relax_column(1 - side)
+
+    relay = (
+        [link(7, xg, xg, at_mate)]
+        + [link(8 + way, yg.at[way], yg.at[way], at_mate) for way in range(2)]
+        + [link(10, cp, cp, at_mate)]
+    )
+
+    @pl.when(side == 1)
+    def _():
+        pack_column(0)
+        pl.semaphore_wait(barrier, 4)
+        to_x = [link(1 + c, xs.at[c], xg.at[1 - c], at_x[c]) for c in range(2)]
+        to_y = [link(3 + way, ys.at[way], yg.at[way], at_y[way]) for way in range(2)]
+        for copy in to_x + to_y:
+            copy.start()
+        for copy in to_x:
+            copy.wait_recv()
+        quarter = lanes_of((8, 128)) // 32
+        for way in range(2):
+            for c in range(2):
+                for k in range(2):
+                    packed = None
+                    for g in range(3):
+                        value = xg[c, 1 - way, k, 8 * g : 8 * g + 8, :]
+                        shift = (32 * g - (96, 0)[way]) % 128
+                        if shift:
+                            value = pltpu.roll(value, shift, 1)
+                        packed = value if packed is None else jnp.where(quarter == g, value, packed)
+                    cs[way, c, k] = packed
+        corners = [link(5 + way, cs.at[way], cp.at[way], at_y[way]) for way in range(2)]
+        for copy in corners:
+            copy.start()
+        relay[0].start()
+        for way in range(2):
+            to_y[way].wait_recv()
+            relay[1 + way].start()
+        for copy in corners:
+            copy.wait_recv()
+        relay[3].start()
+        for copy in to_x + to_y + corners + relay:
+            copy.wait_send()
+
+    @pl.when(side == 0)
+    def _():
+        for copy in relay:
+            copy.wait_recv()
+
+    raw.wait_send()
 
 
 def stream(source, q, row, tiles):
@@ -265,8 +308,8 @@
                 1 - sc, k, tile, pl.ds(mate_far, 19, stride=16), :
             ]
         for g in range(3):
-            low = cp[sc, 0, k]
-            high = cp[sc, 1, k]
+            low = cp[0, sc, k]
+            high = cp[1, sc, k]
             low = pltpu.roll(low, (96 - 32 * g) % 128, 1)
             high = pltpu.roll(high, (-32 * g) % 128, 1) if g else high
             ux[k, 8 * g : 8 * g + 8, :] = jnp.where(lane8 < 64, high, low)
@@ -282,9 +325,9 @@
 
                     def unit(p, lane_to, way=way):
                         if own:
-                            value = yg[sc, way, k, p // 8]
+                            value = yg[way, sc, k, p // 8]
                         else:
-                            value = yg[1 - sc, way, k, p // 8, pl.ds(pl.multiple_of(8 * sc, 8), 8), :]
+                            value = yg[way, 1 - sc, k, p // 8, pl.ds(pl.multiple_of(8 * sc, 8), 8), :]
                         shift = (lane_to - 16 * (p % 8)) % 128
                         return pltpu.roll(value, shift, 1) if shift else value
 
@@ -357,13 +400,14 @@
         in_specs=[HBM] * 3,
         out_specs=[VMEM] * 5,
         scratch_shapes=[
-            pltpu.VMEM((2, 19, 16, 256), F32),
-            pltpu.VMEM((2, 2, 24, 128), F32),
-            pltpu.VMEM((2, 2, 3, 16, 128), F32),
-            pltpu.VMEM((2, 2, 8, 128), F32),
+            pltpu.VMEM((2, 2, 19, 16, 256), F32),
+            pltpu.VMEM((2, 2, 2, 24, 128), F32),
+            pltpu.VMEM((2, 2, 2, 3, 16, 128), F32),
+            pltpu.VMEM((2, 2, 2, 8, 128), F32),
             pltpu.SemaphoreType.DMA((3,)),
             pltpu.SemaphoreType.DMA((11,)),
             pltpu.SemaphoreType.DMA((11,)),
+            pltpu.SemaphoreType.REGULAR,
         ],
         compiler_params=pltpu.CompilerParams(
             collective_id=0, has_side_effects=True, vmem_limit_bytes=8 << 20

time: 35.9 us -> 36.3 us (1.011)
  no operation moved by 1% of the time
where the time goes in v2:
time: 36.3 us; the launch traced here: 36.1 us
  Pallas kernels  36.1 us (99%)
    pallas_call x1, Pallas kernels, shards(): pl.pallas_call(functools.partial(exchange, n_x, n_y), out_shape=[jax.Shap...  33.6 us
    pallas_call x1, Pallas kernels, shards(): pl.pallas_call(advance, out_shape=jax.ShapeDtypeStruct((2, 19, 16, 256),...  2.53 us

profile of v2, /device:TPU:1, one launch (start us, length us, event | category | flops | bytes accessed | tf_op | source)
XLA Modules:
  0.0 36.1 jit_solution(4087289226884921428)
XLA Ops:
  0.0 33.6 %exchange.1 = (f32[2,2,2,304,128]{4,3,2,1,0:T(8,128)S(1)}, f32[2,2,2,24,128]{4,3,2,1,0:T(8,128)S(1)}, f32[2,2,2,3,16,128]{5,4,3,2,1,0:T(8,128)S(1)}, f32[2,2,2,8,128]{4,3,2,1,0:T(8,128)S(1)}, s32[2,2,64]{2,1,0:T(2,128)S(1)}) custom-call(f32[2,19,16,256]{3,2,1,0:T(8,128)} %bitcast.4, s32[16,2,64]{2,1,0:T(2,128)} %bitcast.5, s32[16,2,64]{2,1,0:T(2,128)} %bitcast.6), custom_call_target="tpu_custom_call" | custom-call | tf_op jit(solution)/shard_map/exchange/pallas_call | solution.py:396
  33.6 2.5 %advance.1 = f32[2,19,16,256]{3,2,1,0:T(8,128)} custom-call(f32[2,2,2,304,128]{4,3,2,1,0:T(8,128)S(1)} %get-tuple-element.10.col, f32[2,2,2,24,128]{4,3,2,1,0:T(8,128)S(1)} %get-tuple-element.11.xg, f32[2,2,2,3,16,128]{5,4,3,2,1,0:T(8,128)S(1)} %get-tuple-element.12.yg, f32[2,2,2,8,128]{4,3,2,1,0:T(8,128)S(1)} %get-tuple-element.13.cp, ...), custom_call_target="tpu_custom_call" | custom-call | tf_op jit(solution)/shard_map/advance/pallas_call | solution.py:417

commit v3 on v2

--- a/solution.py
+++ b/solution.py
@@ -74,23 +74,31 @@
 
 def exchange(
     n_x, n_y, pop, live, move, col, xg, yg, cp, tab,
-    fbuf, xs, ys, cs, in_sem, send_sem, recv_sem, ready,
+    fbuf, xs, ys, cs, in_sem, send_sem, recv_sem, allowed,
 ):
     me_x, me_y = lax.axis_index("bx"), lax.axis_index("by")
     side = lax.rem(me_x, 2)
     base = me_x - side
+    hub = base + 1
     at_mate = (base + 1 - side, me_y)
-    at_x = (
-        (lax.rem(base + n_x - 1, n_x), me_y),
-        (lax.rem(base + 3, n_x), me_y),
-    )
-    at_y = ((base + 1, lax.rem(me_y + 1, n_y)), (base + 1, lax.rem(me_y + n_y - 1, n_y)))
+    prev_hub = lax.rem(base + n_x - 1, n_x)
+    next_hub = lax.rem(base + 3, n_x)
+    next_zero = lax.rem(base + 2, n_x)
+    rows_y = (lax.rem(me_y + 1, n_y), lax.rem(me_y + n_y - 1, n_y))
     barrier = pltpu.get_barrier_semaphore()
 
+    def greet(semaphore, devices):
+        for device in devices:
+            pl.semaphore_signal(semaphore, inc=1, device_id=device, device_id_type=MESH)
+
     @pl.when(side == 1)
     def _():
-        for device in at_x + at_y + (at_mate,):
-            pl.semaphore_signal(barrier, inc=1, device_id=device, device_id_type=MESH)
+        around = (me_y,) + rows_y
+        greet(barrier, [(prev_hub, y) for y in around] + [(hub, y) for y in rows_y] + [(next_zero, y) for y in around])
+
+    @pl.when(side == 0)
+    def _():
+        greet(barrier, [at_mate])
 
     load_pop = pltpu.make_async_copy(pop, fbuf.at[side], in_sem.at[0])
     load_live = pltpu.make_async_copy(live.at[me_y], tab.at[0], in_sem.at[1])
@@ -110,12 +118,16 @@
         )
 
     raw = link(0, pop, fbuf.at[side], at_mate)
-
-    @pl.when(side == 0)
-    def _():
-        pl.semaphore_wait(barrier, 1)
-        pl.semaphore_signal(ready, inc=1, device_id=at_mate, device_id_type=MESH)
-        raw.start()
+    high = link(1, xs.at[1], xg.at[0], (next_hub, me_y))
+    low = link(2, xs.at[0], xg.at[1], (prev_hub, me_y))
+    high_corner = [link(3 + w, cs.at[w, 1], cp.at[w, 0], (next_hub, rows_y[w])) for w in range(2)]
+    low_corner = [link(5 + w, cs.at[w, 0], cp.at[w, 1], (prev_hub, rows_y[w])) for w in range(2)]
+    face = [
+        [link(7 + 2 * w + c, ys.at[w, c], yg.at[w, c], (hub, rows_y[w])) for w in range(2)] for c in range(2)
+    ]
+    relay_x = link(11, xg, xg, at_mate)
+    relay_y = [link(12 + w, yg.at[w], yg.at[w], at_mate) for w in range(2)]
+    relay_c = [link(14 + w, cp.at[w], cp.at[w], at_mate) for w in range(2)]
 
     load_live.wait()
     load_move.wait()
@@ -146,8 +158,9 @@
             lax.fori_loop(0, 4, relax, 0)
 
     group = lanes_of((16, 128)) // 16
-
-    def pack_column(c):
+    quarter = lanes_of((8, 128)) // 32
+
+    def pack_x(c):
         near, far = 15 * c, 1 + 13 * c
         for tile in range(2):
             for k in range(2):
@@ -155,7 +168,18 @@
                 xs[c, tile, k, 0:19, :] = own[pl.ds(near, 19, stride=16), :]
                 xs[c, tile, k, 19:20, :] = own[pl.ds((2 - c) * 16 + far, 1), :]
                 xs[c, tile, k, 20:24, :] = own[pl.ds((8 - c) * 16 + far, 4, stride=32), :]
-
+        for way in range(2):
+            for k in range(2):
+                packed = None
+                for g in range(3):
+                    value = xs[c, 1 - way, k, 8 * g : 8 * g + 8, :]
+                    shift = (32 * g - (96, 0)[way]) % 128
+                    if shift:
+                        value = pltpu.roll(value, shift, 1)
+                    packed = value if packed is None else jnp.where(quarter == g, value, packed)
+                cs[way, c, k] = packed
+
+    def pack_y(c):
         def pack(k, carry):
             for way in range(2):
                 tile, first_lane, second_lane = ((1, 112, 96), (0, 0, 16))[way]
@@ -178,58 +202,50 @@
 
     @pl.when(side == 1)
     def _():
-        pack_column(1)
-        pl.semaphore_wait(ready, 1)
+        pack_x(1)
+        pack_y(1)
+        pl.semaphore_wait(barrier, 6)
+        greet(allowed, [at_mate])
+        for copy in high_corner + face[1] + [high, raw]:
+            copy.start()
+
+    @pl.when(side == 0)
+    def _():
+        pack_x(0)
+        pl.semaphore_wait(allowed, 1)
         raw.start()
+        pl.semaphore_wait(barrier, 3)
+        for copy in low_corner + [low]:
+            copy.start()
 
     raw.wait_recv()
     relax_column(1 - side)
 
-    relay = (
-        [link(7, xg, xg, at_mate)]
-        + [link(8 + way, yg.at[way], yg.at[way], at_mate) for way in range(2)]
-        + [link(10, cp, cp, at_mate)]
-    )
-
     @pl.when(side == 1)
     def _():
-        pack_column(0)
-        pl.semaphore_wait(barrier, 4)
-        to_x = [link(1 + c, xs.at[c], xg.at[1 - c], at_x[c]) for c in range(2)]
-        to_y = [link(3 + way, ys.at[way], yg.at[way], at_y[way]) for way in range(2)]
-        for copy in to_x + to_y:
+        pack_y(0)
+        for copy in face[0]:
             copy.start()
-        for copy in to_x:
+        high.wait_recv()
+        low.wait_recv()
+        relay_x.start()
+        for w in range(2):
+            face[1][w].wait_recv()
+            face[0][w].wait_recv()
+            relay_y[w].start()
+        for w in range(2):
+            high_corner[w].wait_recv()
+            low_corner[w].wait_recv()
+            relay_c[w].start()
+        for copy in high_corner + face[0] + face[1] + [high, relay_x] + relay_y + relay_c:
+            copy.wait_send()
+
+    @pl.when(side == 0)
+    def _():
+        for copy in [relay_x] + relay_y + relay_c:
             copy.wait_recv()
-        quarter = lanes_of((8, 128)) // 32
-        for way in range(2):
-            for c in range(2):
-                for k in range(2):
-                    packed = None
-                    for g in range(3):
-                        value = xg[c, 1 - way, k, 8 * g : 8 * g + 8, :]
-                        shift = (32 * g - (96, 0)[way]) % 128
-                        if shift:
-                            value = pltpu.roll(value, shift, 1)
-                        packed = value if packed is None else jnp.where(quarter == g, value, packed)
-                    cs[way, c, k] = packed
-        corners = [link(5 + way, cs.at[way], cp.at[way], at_y[way]) for way in range(2)]
-        for copy in corners:
-            copy.start()
-        relay[0].start()
-        for way in range(2):
-            to_y[way].wait_recv()
-            relay[1 + way].start()
-        for copy in corners:
-            copy.wait_recv()
-        relay[3].start()
-        for copy in to_x + to_y + corners + relay:
+        for copy in low_corner + [low]:
             copy.wait_send()
-
-    @pl.when(side == 0)
-    def _():
-        for copy in relay:
-            copy.wait_recv()
 
     raw.wait_send()
 
@@ -405,8 +421,8 @@
             pltpu.VMEM((2, 2, 2, 3, 16, 128), F32),
             pltpu.VMEM((2, 2, 2, 8, 128), F32),
             pltpu.SemaphoreType.DMA((3,)),
-            pltpu.SemaphoreType.DMA((11,)),
-            pltpu.SemaphoreType.DMA((11,)),
+            pltpu.SemaphoreType.DMA((16,)),
+            pltpu.SemaphoreType.DMA((16,)),
             pltpu.SemaphoreType.REGULAR,
         ],
         compiler_params=pltpu.CompilerParams(

time: 36.3 us -> 32.7 us (0.901)
  Pallas kernels: 36.1 us -> 32.6 us
    pallas_call x1, Pallas kernels: 33.6 us -> 30 us  [shards(): pl.pallas_call(functools.partial(exchange, n_x, n_y), out_shape=[jax.Shap...]
where the time goes in v3:
time: 32.7 us; the launch traced here: 32.6 us
  Pallas kernels  32.6 us (100%)
    pallas_call x1, Pallas kernels, shards(): pl.pallas_call(functools.partial(exchange, n_x, n_y), out_shape=[jax.Shap...  30 us
    pallas_call x1, Pallas kernels, shards(): pl.pallas_call(advance, out_shape=jax.ShapeDtypeStruct((2, 19, 16, 256),...  2.55 us

profile of v3, /device:TPU:1, one launch (start us, length us, event | category | flops | bytes accessed | tf_op | source)
XLA Modules:
  0.0 32.6 jit_solution(2231139907589767930)
XLA Ops:
  0.0 30.0 %exchange.1 = (f32[2,2,2,304,128]{4,3,2,1,0:T(8,128)S(1)}, f32[2,2,2,24,128]{4,3,2,1,0:T(8,128)S(1)}, f32[2,2,2,3,16,128]{5,4,3,2,1,0:T(8,128)S(1)}, f32[2,2,2,8,128]{4,3,2,1,0:T(8,128)S(1)}, s32[2,2,64]{2,1,0:T(2,128)S(1)}) custom-call(f32[2,19,16,256]{3,2,1,0:T(8,128)} %bitcast.4, s32[16,2,64]{2,1,0:T(2,128)} %bitcast.5, s32[16,2,64]{2,1,0:T(2,128)} %bitcast.6), custom_call_target="tpu_custom_call" | custom-call | tf_op jit(solution)/shard_map/exchange/pallas_call | solution.py:412
  30.0 2.5 %advance.1 = f32[2,19,16,256]{3,2,1,0:T(8,128)} custom-call(f32[2,2,2,304,128]{4,3,2,1,0:T(8,128)S(1)} %get-tuple-element.10.col, f32[2,2,2,24,128]{4,3,2,1,0:T(8,128)S(1)} %get-tuple-element.11.xg, f32[2,2,2,3,16,128]{5,4,3,2,1,0:T(8,128)S(1)} %get-tuple-element.12.yg, f32[2,2,2,8,128]{4,3,2,1,0:T(8,128)S(1)} %get-tuple-element.13.cp, ...), custom_call_target="tpu_custom_call" | custom-call | tf_op jit(solution)/shard_map/advance/pallas_call | solution.py:433

commit v4 on v3

--- a/solution.py
+++ b/solution.py
@@ -203,17 +203,21 @@
     @pl.when(side == 1)
     def _():
         pack_x(1)
-        pack_y(1)
         pl.semaphore_wait(barrier, 6)
         greet(allowed, [at_mate])
-        for copy in high_corner + face[1] + [high, raw]:
+        for copy in high_corner + [high]:
             copy.start()
+        pack_y(1)
+        for copy in face[1] + [raw]:
+            copy.start()
 
     @pl.when(side == 0)
     def _():
         pack_x(0)
+        pack_y(0)
         pl.semaphore_wait(allowed, 1)
-        raw.start()
+        for copy in face[0] + [raw]:
+            copy.start()
         pl.semaphore_wait(barrier, 3)
         for copy in low_corner + [low]:
             copy.start()
@@ -223,9 +227,6 @@
 
     @pl.when(side == 1)
     def _():
-        pack_y(0)
-        for copy in face[0]:
-            copy.start()
         high.wait_recv()
         low.wait_recv()
         relay_x.start()
@@ -237,14 +238,14 @@
             high_corner[w].wait_recv()
             low_corner[w].wait_recv()
             relay_c[w].start()
-        for copy in high_corner + face[0] + face[1] + [high, relay_x] + relay_y + relay_c:
+        for copy in high_corner + face[1] + [high, relay_x] + relay_y + relay_c:
             copy.wait_send()
 
     @pl.when(side == 0)
     def _():
         for copy in [relay_x] + relay_y + relay_c:
             copy.wait_recv()
-        for copy in low_corner + [low]:
+        for copy in low_corner + face[0] + [low]:
             copy.wait_send()
 
     raw.wait_send()

time: 32.7 us -> 31.8 us (0.972)
  Pallas kernels: 32.6 us -> 31.6 us
    pallas_call x1, Pallas kernels: 30 us -> 29 us  [shards(): pl.pallas_call(functools.partial(exchange, n_x, n_y), out_shape=[jax.Shap...]
where the time goes in v4:
time: 31.8 us; the launch traced here: 31.6 us
  Pallas kernels  31.6 us (99%)
    pallas_call x1, Pallas kernels, shards(): pl.pallas_call(functools.partial(exchange, n_x, n_y), out_shape=[jax.Shap...  29 us
    pallas_call x1, Pallas kernels, shards(): pl.pallas_call(advance, out_shape=jax.ShapeDtypeStruct((2, 19, 16, 256),...  2.53 us

profile of v4, /device:TPU:1, one launch (start us, length us, event | category | flops | bytes accessed | tf_op | source)
XLA Modules:
  0.0 31.6 jit_solution(16060317360589994846)
XLA Ops:
  0.0 29.0 %exchange.1 = (f32[2,2,2,304,128]{4,3,2,1,0:T(8,128)S(1)}, f32[2,2,2,24,128]{4,3,2,1,0:T(8,128)S(1)}, f32[2,2,2,3,16,128]{5,4,3,2,1,0:T(8,128)S(1)}, f32[2,2,2,8,128]{4,3,2,1,0:T(8,128)S(1)}, s32[2,2,64]{2,1,0:T(2,128)S(1)}) custom-call(f32[2,19,16,256]{3,2,1,0:T(8,128)} %bitcast.4, s32[16,2,64]{2,1,0:T(2,128)} %bitcast.5, s32[16,2,64]{2,1,0:T(2,128)} %bitcast.6), custom_call_target="tpu_custom_call" | custom-call | tf_op jit(solution)/shard_map/exchange/pallas_call | solution.py:413
  29.1 2.5 %advance.1 = f32[2,19,16,256]{3,2,1,0:T(8,128)} custom-call(f32[2,2,2,304,128]{4,3,2,1,0:T(8,128)S(1)} %get-tuple-element.10.col, f32[2,2,2,24,128]{4,3,2,1,0:T(8,128)S(1)} %get-tuple-element.11.xg, f32[2,2,2,3,16,128]{5,4,3,2,1,0:T(8,128)S(1)} %get-tuple-element.12.yg, f32[2,2,2,8,128]{4,3,2,1,0:T(8,128)S(1)} %get-tuple-element.13.cp, ...), custom_call_target="tpu_custom_call" | custom-call | tf_op jit(solution)/shard_map/advance/pallas_call | solution.py:434

commit v5 on v4

--- a/solution.py
+++ b/solution.py
@@ -73,8 +73,8 @@
 
 
 def exchange(
-    n_x, n_y, pop, live, move, col, xg, yg, cp, tab,
-    fbuf, xs, ys, cs, in_sem, send_sem, recv_sem, allowed,
+    n_x, n_y, pop, live, move, ext, tab,
+    col, xg, yg, cp, fbuf, xs, ys, cs, ux, in_sem, send_sem, recv_sem, allowed,
 ):
     me_x, me_y = lax.axis_index("bx"), lax.axis_index("by")
     side = lax.rem(me_x, 2)
@@ -225,26 +225,140 @@
     raw.wait_recv()
     relax_column(1 - side)
 
+    def pair(table, device):
+        row = tab[table]
+        one = jnp.sum(jnp.where(lanes_of(row.shape) == device, row, 0).astype(F32), axis=1, keepdims=True)
+        return one[0:1, :] + one[1:2, :]
+
+    swap = jnp.where(pair(0, me_x) < 0.5, jnp.where(pair(1, base + 1 - side) > 0.5, 1.0, 0.0), 0.0)
+    column = jnp.abs(swap - side.astype(F32))
+
+    def first_or_second(first, second):
+        return jnp.where(jnp.broadcast_to(column, first.shape) < 0.5, first, second)
+
+    def every(start, count=19, stride=32):
+        return pl.ds(start, count, stride=stride)
+
+    def gather_columns(k, carry):
+        for tile in range(2):
+            for q in range(19):
+                rows = slice(q * 16, q * 16 + 16)
+                ext[k, tile, q * 32 + 8 : q * 32 + 24, :] = first_or_second(
+                    col[0, k, tile, rows, :], col[1, k, tile, rows, :]
+                )
+        return carry
+
+    lax.fori_loop(0, 2, gather_columns, 0)
+
     @pl.when(side == 1)
     def _():
         high.wait_recv()
         low.wait_recv()
         relay_x.start()
+
+    @pl.when(side == 0)
+    def _():
+        relay_x.wait_recv()
+
+    def place_ghost(k, tile, c, planes, inner_near, inner_far):
+        near, far = ((7, 6), (24, 25))[c]
+
+        def choose(outer, inner):
+            return first_or_second(outer, inner) if c == 0 else first_or_second(inner, outer)
+
+        ext[k, tile, every(near), :] = choose(planes[0:19, :], inner_near)
+        ext[k, tile, every(far), :] = inner_far
+        one = pl.ds((1 + c) * 32 + far, 1)
+        ext[k, tile, one, :] = choose(planes[19:20, :], ext[k, tile, one, :])
+        four = every((7 + c) * 32 + far, 4, 64)
+        ext[k, tile, four, :] = choose(planes[20:24, :], ext[k, tile, four, :])
+
+    def gather_x(k, carry):
+        for tile in range(2):
+            for c in range(2):
+                near, far = ((15, 14), (0, 1))[c]
+                place_ghost(
+                    k, tile, c, xg.at[c, tile, k],
+                    col[c, k, tile, every(near, stride=16), :], col[c, k, tile, every(far, stride=16), :],
+                )
+        return carry
+
+    lax.fori_loop(0, 2, gather_x, 0)
+
+    @pl.when(side == 1)
+    def _():
         for w in range(2):
             face[1][w].wait_recv()
             face[0][w].wait_recv()
             relay_y[w].start()
+
+    @pl.when(side == 0)
+    def _():
+        for copy in relay_y:
+            copy.wait_recv()
+
+    def unpack(units, q, rows):
+        lane = lanes_of((rows, 128))
+        parts = []
+        for way in range(2):
+            near_lane, far_lane = ((112, 96), (0, 16))[way]
+
+            def unit(p, lane_to, way=way):
+                shift = (lane_to - 16 * (p % 8)) % 128
+                value = units[way][p // 8]
+                return pltpu.roll(value, shift, 1) if shift else value
+
+            value = unit(q, near_lane)
+            if q in RING_Y[way]:
+                far = unit(19 + RING_Y[way].index(q), far_lane)
+                value = jnp.where(lane // 16 == near_lane // 16, value, far)
+            parts.append(value)
+        return jnp.where(lane < 64, parts[1], parts[0])
+
+    def gather_y(k, carry):
+        units = [[first_or_second(yg[w, 0, k, g], yg[w, 1, k, g]) for g in range(3)] for w in range(2)]
+        for q in range(19):
+            ext[k, 2, q * 32 + 8 : q * 32 + 24, :] = unpack(units, q, 16)
+        for c in range(2):
+            rows = (slice(8, 16), slice(0, 8))[c]
+            units = [[yg[w, c, k, g, rows, :] for g in range(3)] for w in range(2)]
+            for q in range(19):
+                start = q * 32 + 24 * c
+                ext[k, 2, start : start + 8, :] = unpack(units, q, 8)
+        return carry
+
+    lax.fori_loop(0, 2, gather_y, 0)
+
+    @pl.when(side == 1)
+    def _():
         for w in range(2):
             high_corner[w].wait_recv()
             low_corner[w].wait_recv()
             relay_c[w].start()
+
+    @pl.when(side == 0)
+    def _():
+        for copy in relay_c:
+            copy.wait_recv()
+
+    lane8 = lanes_of((8, 128))
+    for k in range(2):
+        for c in range(2):
+            for g in range(3):
+                up = pltpu.roll(cp[0, c, k], (96 - 32 * g) % 128, 1)
+                down = cp[1, c, k]
+                down = pltpu.roll(down, (-32 * g) % 128, 1) if g else down
+                ux[k, c, 8 * g : 8 * g + 8, :] = jnp.where(lane8 < 64, down, up)
+            near, far = ((7, 6), (24, 25))[c]
+            place_ghost(k, 2, c, ux.at[k, c], ext[k, 2, every(near), :], ext[k, 2, every(far), :])
+
+    @pl.when(side == 1)
+    def _():
         for copy in high_corner + face[1] + [high, relay_x] + relay_y + relay_c:
             copy.wait_send()
 
     @pl.when(side == 0)
     def _():
-        for copy in [relay_x] + relay_y + relay_c:
-            copy.wait_recv()
         for copy in low_corner + face[0] + [low]:
             copy.wait_send()
 
@@ -284,7 +398,7 @@
     return moved
 
 
-def advance(col, xg, yg, cp, tab, out, ext, nxt, ux, fs):
+def advance(ext, tab, out, nxt, fs):
     me_x = lax.axis_index("bx")
     side = lax.rem(me_x, 2)
     mate = me_x + 1 - 2 * side
@@ -301,63 +415,6 @@
     chosen = [
         jnp.where(swap, arriving[k], own_live[k] * (1.0 - own_moving[k])) > 0.5 for k in range(2)
     ]
-    sc = jnp.where(swap, 1 - side, side)
-
-    outer_near, outer_far = 7 + 17 * sc, 6 + 19 * sc
-    inner_near, inner_far = 24 - 17 * sc, 25 - 19 * sc
-    mate_near, mate_far = 15 * sc, 1 + 13 * sc
-    lane8 = lanes_of((8, 128))
-
-    def place_outer(k, tile, planes):
-        ext[k, tile, pl.ds(outer_near, 19, stride=32), :] = planes[0:19, :]
-        ext[k, tile, pl.ds((1 + sc) * 32 + outer_far, 1), :] = planes[19:20, :]
-        ext[k, tile, pl.ds((7 + sc) * 32 + outer_far, 4, stride=64), :] = planes[20:24, :]
-
-    for k in range(2):
-        for tile in range(2):
-            for q in range(19):
-                ext[k, tile, q * 32 + 8 : q * 32 + 24, :] = col[sc, k, tile, q * 16 : q * 16 + 16, :]
-            place_outer(k, tile, xg.at[sc, tile, k])
-            ext[k, tile, pl.ds(inner_near, 19, stride=32), :] = col[
-                1 - sc, k, tile, pl.ds(mate_near, 19, stride=16), :
-            ]
-            ext[k, tile, pl.ds(inner_far, 19, stride=32), :] = col[
-                1 - sc, k, tile, pl.ds(mate_far, 19, stride=16), :
-            ]
-        for g in range(3):
-            low = cp[0, sc, k]
-            high = cp[1, sc, k]
-            low = pltpu.roll(low, (96 - 32 * g) % 128, 1)
-            high = pltpu.roll(high, (-32 * g) % 128, 1) if g else high
-            ux[k, 8 * g : 8 * g + 8, :] = jnp.where(lane8 < 64, high, low)
-        place_outer(k, 2, ux.at[k])
-
-        for own in range(2):
-            rows = 16 if own else 8
-            lane = lanes_of((rows, 128))
-            for q in range(19):
-                parts = []
-                for way in range(2):
-                    near_lane, far_lane = ((112, 96), (0, 16))[way]
-
-                    def unit(p, lane_to, way=way):
-                        if own:
-                            value = yg[way, sc, k, p // 8]
-                        else:
-                            value = yg[way, 1 - sc, k, p // 8, pl.ds(pl.multiple_of(8 * sc, 8), 8), :]
-                        shift = (lane_to - 16 * (p % 8)) % 128
-                        return pltpu.roll(value, shift, 1) if shift else value
-
-                    value = unit(q, near_lane)
-                    if q in RING_Y[way]:
-                        far = unit(19 + RING_Y[way].index(q), far_lane)
-                        value = jnp.where(lane // 16 == near_lane // 16, value, far)
-                    parts.append(value)
-                value = jnp.where(lane < 64, parts[1], parts[0])
-                if own:
-                    ext[k, 2, q * 32 + 8 : q * 32 + 24, :] = value
-                else:
-                    ext[k, 2, pl.ds(pl.multiple_of(q * 32 + 24 - 24 * sc, 8), 8), :] = value
 
     def arrive(source, stride, base, q, row, tiles):
         moved = stream(source, q, q * stride + base + row - VELOCITIES[q][0], tiles)
@@ -409,37 +466,41 @@
             jnp.transpose(moving, (1, 2, 0)),
         )
     )
-    shapes = [(2, 2, 2, 304, 128), (2, 2, 2, 24, 128), (2, 2, 2, 3, 16, 128), (2, 2, 2, 8, 128)]
     parts = pl.pallas_call(
         functools.partial(exchange, n_x, n_y),
-        out_shape=[jax.ShapeDtypeStruct(shape, F32) for shape in shapes]
-        + [jax.ShapeDtypeStruct((2, 2, n_x), jnp.int32)],
+        out_shape=[
+            jax.ShapeDtypeStruct((2, 3, 19 * 32, 128), F32),
+            jax.ShapeDtypeStruct((2, 2, n_x), jnp.int32),
+        ],
         in_specs=[HBM] * 3,
-        out_specs=[VMEM] * 5,
+        out_specs=[VMEM] * 2,
         scratch_shapes=[
+            pltpu.VMEM((2, 2, 2, 304, 128), F32),
+            pltpu.VMEM((2, 2, 2, 24, 128), F32),
+            pltpu.VMEM((2, 2, 2, 3, 16, 128), F32),
+            pltpu.VMEM((2, 2, 2, 8, 128), F32),
             pltpu.VMEM((2, 2, 19, 16, 256), F32),
             pltpu.VMEM((2, 2, 2, 24, 128), F32),
             pltpu.VMEM((2, 2, 2, 3, 16, 128), F32),
             pltpu.VMEM((2, 2, 2, 8, 128), F32),
+            pltpu.VMEM((2, 2, 24, 128), F32),
             pltpu.SemaphoreType.DMA((3,)),
             pltpu.SemaphoreType.DMA((16,)),
             pltpu.SemaphoreType.DMA((16,)),
             pltpu.SemaphoreType.REGULAR,
         ],
         compiler_params=pltpu.CompilerParams(
-            collective_id=0, has_side_effects=True, vmem_limit_bytes=8 << 20
+            collective_id=0, has_side_effects=True, vmem_limit_bytes=12 << 20
         ),
         name="exchange",
     )(pop, live, move)
     result = pl.pallas_call(
         advance,
         out_shape=jax.ShapeDtypeStruct((2, 19, 16, 256), F32),
-        in_specs=[VMEM] * 5,
+        in_specs=[VMEM] * 2,
         out_specs=VMEM,
         scratch_shapes=[
-            pltpu.VMEM((2, 3, 19 * 32, 128), F32),
             pltpu.VMEM((2, 3, 19 * 24, 128), F32),
-            pltpu.VMEM((2, 24, 128), F32),
             pltpu.VMEM((19, 2, 3, 8, 128), F32),
         ],
         compiler_params=pltpu.CompilerParams(vmem_limit_bytes=12 << 20),

time: 31.8 us -> 31.6 us (level)
    pallas_call x1, Pallas kernels: 2.53 us -> 2.08 us  [shards(): pl.pallas_call(advance, out_shape=jax.ShapeDtypeStruct((2, 19, 16, 256),...]
where the time goes in v5:
time: 31.6 us; the launch traced here: 31.4 us
  Pallas kernels  31.4 us (99%)
    pallas_call x1, Pallas kernels, shards(): pl.pallas_call(functools.partial(exchange, n_x, n_y), out_shape=[jax.Shap...  29.3 us
    pallas_call x1, Pallas kernels, shards(): pl.pallas_call(advance, out_shape=jax.ShapeDtypeStruct((2, 19, 16, 256),...  2.08 us

profile of v5, /device:TPU:1, one launch (start us, length us, event | category | flops | bytes accessed | tf_op | source)
XLA Modules:
  0.0 31.4 jit_solution(5710019320505797577)
XLA Ops:
  0.0 29.3 %exchange.1 = (f32[2,3,608,128]{3,2,1,0:T(8,128)S(1)}, s32[2,2,64]{2,1,0:T(2,128)S(1)}) custom-call(f32[2,19,16,256]{3,2,1,0:T(8,128)} %bitcast.4, s32[16,2,64]{2,1,0:T(2,128)} %bitcast.5, s32[16,2,64]{2,1,0:T(2,128)} %bitcast.6), custom_call_target="tpu_custom_call" | custom-call | tf_op jit(solution)/shard_map/exchange/pallas_call | solution.py:469
  29.3 2.1 %advance.1 = f32[2,19,16,256]{3,2,1,0:T(8,128)} custom-call(f32[2,3,608,128]{3,2,1,0:T(8,128)S(1)} %get-tuple-element.7.ext, s32[2,2,64]{2,1,0:T(2,128)S(1)} %get-tuple-element.8.tab), custom_call_target="tpu_custom_call" | custom-call | tf_op jit(solution)/shard_map/advance/pallas_call | solution.py:497

commit v6 on v5

--- a/solution.py
+++ b/solution.py
@@ -252,41 +252,6 @@
 
     @pl.when(side == 1)
     def _():
-        high.wait_recv()
-        low.wait_recv()
-        relay_x.start()
-
-    @pl.when(side == 0)
-    def _():
-        relay_x.wait_recv()
-
-    def place_ghost(k, tile, c, planes, inner_near, inner_far):
-        near, far = ((7, 6), (24, 25))[c]
-
-        def choose(outer, inner):
-            return first_or_second(outer, inner) if c == 0 else first_or_second(inner, outer)
-
-        ext[k, tile, every(near), :] = choose(planes[0:19, :], inner_near)
-        ext[k, tile, every(far), :] = inner_far
-        one = pl.ds((1 + c) * 32 + far, 1)
-        ext[k, tile, one, :] = choose(planes[19:20, :], ext[k, tile, one, :])
-        four = every((7 + c) * 32 + far, 4, 64)
-        ext[k, tile, four, :] = choose(planes[20:24, :], ext[k, tile, four, :])
-
-    def gather_x(k, carry):
-        for tile in range(2):
-            for c in range(2):
-                near, far = ((15, 14), (0, 1))[c]
-                place_ghost(
-                    k, tile, c, xg.at[c, tile, k],
-                    col[c, k, tile, every(near, stride=16), :], col[c, k, tile, every(far, stride=16), :],
-                )
-        return carry
-
-    lax.fori_loop(0, 2, gather_x, 0)
-
-    @pl.when(side == 1)
-    def _():
         for w in range(2):
             face[1][w].wait_recv()
             face[0][w].wait_recv()
@@ -328,6 +293,41 @@
         return carry
 
     lax.fori_loop(0, 2, gather_y, 0)
+
+    @pl.when(side == 1)
+    def _():
+        high.wait_recv()
+        low.wait_recv()
+        relay_x.start()
+
+    @pl.when(side == 0)
+    def _():
+        relay_x.wait_recv()
+
+    def place_ghost(k, tile, c, planes, inner_near, inner_far):
+        near, far = ((7, 6), (24, 25))[c]
+
+        def choose(outer, inner):
+            return first_or_second(outer, inner) if c == 0 else first_or_second(inner, outer)
+
+        ext[k, tile, every(near), :] = choose(planes[0:19, :], inner_near)
+        ext[k, tile, every(far), :] = inner_far
+        one = pl.ds((1 + c) * 32 + far, 1)
+        ext[k, tile, one, :] = choose(planes[19:20, :], ext[k, tile, one, :])
+        four = every((7 + c) * 32 + far, 4, 64)
+        ext[k, tile, four, :] = choose(planes[20:24, :], ext[k, tile, four, :])
+
+    def gather_x(k, carry):
+        for tile in range(2):
+            for c in range(2):
+                near, far = ((15, 14), (0, 1))[c]
+                place_ghost(
+                    k, tile, c, xg.at[c, tile, k],
+                    col[c, k, tile, every(near, stride=16), :], col[c, k, tile, every(far, stride=16), :],
+                )
+        return carry
+
+    lax.fori_loop(0, 2, gather_x, 0)
 
     @pl.when(side == 1)
     def _():

time: 31.6 us -> 31.1 us (0.984)
  Pallas kernels: 31.4 us -> 30.9 us
    pallas_call x1, Pallas kernels: 29.3 us -> 28.8 us  [shards(): pl.pallas_call(functools.partial(exchange, n_x, n_y), out_shape=[jax.Shap...]
where the time goes in v6:
time: 31.1 us; the launch traced here: 30.9 us
  Pallas kernels  30.9 us (99%)
    pallas_call x1, Pallas kernels, shards(): pl.pallas_call(functools.partial(exchange, n_x, n_y), out_shape=[jax.Shap...  28.8 us
    pallas_call x1, Pallas kernels, shards(): pl.pallas_call(advance, out_shape=jax.ShapeDtypeStruct((2, 19, 16, 256),...  2.08 us

profile of v6, /device:TPU:1, one launch (start us, length us, event | category | flops | bytes accessed | tf_op | source)
XLA Modules:
  0.0 30.9 jit_solution(5598052214717074984)
XLA Ops:
  0.0 28.8 %exchange.1 = (f32[2,3,608,128]{3,2,1,0:T(8,128)S(1)}, s32[2,2,64]{2,1,0:T(2,128)S(1)}) custom-call(f32[2,19,16,256]{3,2,1,0:T(8,128)} %bitcast.4, s32[16,2,64]{2,1,0:T(2,128)} %bitcast.5, s32[16,2,64]{2,1,0:T(2,128)} %bitcast.6), custom_call_target="tpu_custom_call" | custom-call | tf_op jit(solution)/shard_map/exchange/pallas_call | solution.py:469
  28.9 2.1 %advance.1 = f32[2,19,16,256]{3,2,1,0:T(8,128)} custom-call(f32[2,3,608,128]{3,2,1,0:T(8,128)S(1)} %get-tuple-element.7.ext, s32[2,2,64]{2,1,0:T(2,128)S(1)} %get-tuple-element.8.tab), custom_call_target="tpu_custom_call" | custom-call | tf_op jit(solution)/shard_map/advance/pallas_call | solution.py:497
